TPU v7x, 32 devices: a whole 2x2x4 slice. The times are simulated.
32 devices in a mesh: groups: 2 (over y), seq: 4 (over z), head: 4 (over x, core).
Axes of the slice: x: 2, y: 2, z: 4, core: 2. Of those that a mesh axis runs over, the one named last changes fastest.
Arguments:
- queries: bfloat16 [4096, 2048], P(('groups', 'seq'), 'head'), parts along dimension 0, may hold values from -8 to 8
- keys: bfloat16 [4096, 2048], P(('groups', 'seq'), 'head'), parts along dimension 0, may hold values from -8 to 8
- values: bfloat16 [4096, 2048], P(('groups', 'seq'), 'head'), parts along dimension 0, may hold values from -12 to 12
- w_out: bfloat16 [2048, 2048], replicated, may hold values from -0.125 to 0.125
Outputs:
- projected: bfloat16 [4096, 2048], P(('groups', 'seq', 'head')), parts along dimension 0
There are 2 independent parts, one for each index of `groups`. A program takes and returns all parts, laid end to end along the dimension named above; an argument that names none is the same for every part. Nothing has to cross between parts.
All inputs are finite; a program needn't handle non-finite values.
Results may differ from a plain program's by a relative error of at most 0.005.
Values may be sent and summed in bfloat16 or wider, within the bound.
A program may use at most 128 MiB of HBM per device.

v0:
```python
import functools
import math

import jax
import jax.numpy as jnp
from jax import lax
from jax.experimental import pallas as pl
from jax.experimental.pallas import tpu as pltpu
from jax.sharding import PartitionSpec as P

HD = 128
WINDOW = 2048
MESH = pl.DeviceIdType.MESH
F32 = jnp.float32
BF16 = jnp.bfloat16
RATE = math.log2(math.e) / math.sqrt(HD)
FLOOR = -1e30


def dot_nt(a, b):
    return lax.dot_general(a, b, (((1,), (1,)), ((), ())), preferred_element_type=F32)


def dot_tn(a, b):
    return lax.dot_general(a, b, (((0,), (0,)), ((), ())), preferred_element_type=F32)


def kernel(
    peers, q_hbm, k_hbm, v_hbm, w_hbm, out_ref, q_ref, k_ref, v_ref,
    w_ref, summed, kbuf, vbuf, qbuf, o_send, o_recv, t_send, t_recv, s_send, s_recv, acc, lin, stat,
    mixed, gathered, in_sem, w_sem, kv_tx, kv_rx, q_tx, q_rx, o_tx, o_rx, t_tx, t_rx, s_tx, s_rx, m_tx, m_rx,
):
    seq = lax.axis_index("seq")
    here = lax.axis_index("head")
    blocks = lax.axis_size("seq")
    length, width = q_ref.shape
    heads = width // HD
    share = length // peers

    loads = [
        pltpu.make_async_copy(source, target, in_sem.at[i])
        for i, (source, target) in enumerate(((q_hbm, q_ref), (k_hbm, k_ref), (v_hbm, v_ref)))
    ]
    for load in loads:
        load.start()

    def load_w(h, peer):
        return pltpu.make_async_copy(
            w_hbm.at[pl.ds(pl.multiple_of(peer * width + h * HD, HD), HD), :],
            w_ref.at[h, pl.ds(peer * HD, HD), :],
            w_sem.at[h, peer],
        )

    def load_head(h):
        for peer in range(peers):
            load_w(h, peer).start()


    barrier = pltpu.get_barrier_semaphore()
    for step in range(1, blocks):
        pl.semaphore_signal(
            barrier, inc=1, device_id={"seq": lax.rem(seq + step, blocks)}, device_id_type=MESH
        )
    for step in range(1, peers):
        pl.semaphore_signal(
            barrier, inc=1, device_id={"head": lax.rem(here + step, peers)}, device_id_type=MESH
        )
    pl.semaphore_wait(barrier, blocks - 1 + peers - 1)
    for load in loads:
        load.wait()
    lax.fori_loop(0, heads, lambda h, c: (load_head(h), c)[1], 0)

    def cols(h):
        return pl.ds(pl.multiple_of(h * HD, HD), HD)

    def remote(source, target, tx, rx, device):
        return pltpu.make_async_remote_copy(
            src_ref=source, dst_ref=target, send_sem=tx, recv_sem=rx,
            device_id=device, device_id_type=MESH,
        )

    def key_copy(h):
        return remote(
            k_ref.at[:, cols(h)], kbuf.at[:, cols(h)], kv_tx.at[0, h], kv_rx.at[0, h], {"seq": 1}
        )

    def value_copy(h):
        return remote(
            v_ref.at[:, cols(h)], vbuf.at[:, cols(h)], kv_tx.at[1, h], kv_rx.at[1, h], {"seq": 1}
        )

    def query_copy(h, slot, target):
        return remote(
            q_ref.at[:, cols(h)], qbuf.at[slot, :, cols(h)],
            q_tx.at[slot, h], q_rx.at[slot, h], {"seq": target},
        )

    def relay_copy(h):
        return remote(
            qbuf.at[1, :, cols(h)], qbuf.at[1, :, cols(h)], q_tx.at[1, h], q_rx.at[1, h], {"seq": 1}
        )

    def part_copies(h, out_slot, in_slot, target):
        return (
            remote(
                t_send.at[out_slot, h], t_recv.at[in_slot, h],
                t_tx.at[out_slot, h], t_rx.at[in_slot, h], {"seq": target},
            ),
            remote(
                o_send.at[out_slot, h], o_recv.at[in_slot, h],
                o_tx.at[out_slot, h], o_rx.at[in_slot, h], {"seq": target},
            ),
        )

    def state_copy(h, tx_slot, in_slot, target):
        return remote(
            s_send.at[h], s_recv.at[in_slot, h], s_tx.at[tx_slot, h], s_rx.at[in_slot, h],
            {"seq": target},
        )

    def prefix_copy(h):
        return remote(
            s_recv.at[0, h], s_recv.at[0, h], s_tx.at[1, h], s_rx.at[0, h], {"seq": 3}
        )

    def mixed_copy(h, step):
        target = lax.rem(here + step, peers)
        return remote(
            mixed.at[pl.ds(pl.multiple_of(h * HD, HD), HD), pl.ds(pl.multiple_of(target * share, HD), share)],
            gathered.at[h, pl.ds(pl.multiple_of(here * HD, HD), HD), :],
            m_tx.at[h, step], m_rx.at[h, step], {"head": target},
        )

    def loop(body):
        lax.fori_loop(0, heads, lambda h, c: (body(h), c)[1], 0)

    causal = lax.broadcasted_iota(jnp.int32, (length, length), 0) <= lax.broadcasted_iota(
        jnp.int32, (length, length), 1
    )

    def own(h):
        query, key, value = q_ref[:, cols(h)], k_ref[:, cols(h)], v_ref[:, cols(h)]
        scores = dot_nt(key, query)
        kept = jnp.where(causal, scores, 0.0)
        coarse = kept.astype(BF16)
        fine = (kept - coarse.astype(F32)).astype(BF16)
        lin[h] = dot_tn(value, coarse) + dot_tn(value, fine)
        scores = jnp.where(causal, scores, FLOOR)
        top = jnp.max(scores, axis=0, keepdims=True)
        expo = jnp.exp2((scores - top) * RATE)
        stat[h, 0:1, :] = top
        stat[h, 1:2, :] = jnp.sum(expo, axis=0, keepdims=True)
        acc[h] = dot_tn(value, expo.astype(BF16))

    def part(query, pairs):
        scores = [dot_nt(key, query) for key, _ in pairs]
        top = functools.reduce(jnp.maximum, [jnp.max(s, axis=0, keepdims=True) for s in scores])
        expo = [jnp.exp2((s - top) * RATE) for s in scores]
        total = sum(jnp.sum(e, axis=0, keepdims=True) for e in expo)
        output = sum(dot_tn(value, e.astype(BF16)) for e, (_, value) in zip(expo, pairs))
        return top, total, output

    def emit(h, slot, top, total, output):
        row = lax.broadcasted_iota(jnp.int32, t_send.shape[2:], 0)
        t_send[slot, h] = jnp.where(row == 0, top, total)
        o_send[slot, h] = (output / total).astype(BF16)

    def merged(h, others):
        tops = [stat[h, 0:1, :]] + [o[0] for o in others]
        top = functools.reduce(jnp.maximum, tops)
        scale = jnp.exp2((tops[0] - top) * RATE)
        total = scale * stat[h, 1:2, :]
        output = scale * acc[h]
        for other_top, other_total, other, normal in others:
            scale = jnp.exp2((other_top - top) * RATE)
            total += scale * other_total
            output += (scale * other_total if normal else scale) * other
        return output / total

    def received(h, slot):
        return t_recv[slot, h, 0:1, :], t_recv[slot, h, 1:2, :], o_recv[slot, h].astype(F32), True

    def finish(h, windowed, linear):
        square = jnp.mean(linear * linear, axis=0, keepdims=True)
        rows = pl.ds(pl.multiple_of(h * HD, HD), HD)
        mixed[rows, :] = (linear / jnp.sqrt(square + 1e-06) + windowed).astype(BF16)
        for step in range(1, peers):
            mixed_copy(h, step).start()
        gathered[h, pl.ds(pl.multiple_of(here * HD, HD), HD), :] = mixed[
            rows, pl.ds(pl.multiple_of(here * share, HD), share)
        ]

    tile = math.gcd(w_ref.shape[2], 512)

    def project(h):
        for peer in range(peers):
            load_w(h, peer).wait()
        for step in range(1, peers):
            mixed_copy(h, step).wait()
        left = gathered[h].T

        @pl.loop(0, w_ref.shape[2] // tile)
        def _(index):
            part_cols = pl.ds(pl.multiple_of(index * tile, tile), tile)
            summed[:, part_cols] += jnp.dot(
                left, w_ref[h, :, part_cols], preferred_element_type=F32
            )

    def project_before(h):
        @pl.when(h > 0)
        def _():
            project(h - 1)

    summed[...] = jnp.zeros_like(summed)

    @pl.when(seq == 0)
    def _():
        def send(h):
            key_copy(h).start()
            value_copy(h).start()

        def work(h):
            own(h)
            finish(h, acc[h] / stat[h, 1:2, :], lin[h])
            project_before(h)

        def drain(h):
            key_copy(h).wait_send()
            value_copy(h).wait_send()

        loop(send)
        loop(work)
        loop(drain)

    @pl.when(seq == 1)
    def _():
        def work(h):
            project_before(h)
            key_copy(h).wait_recv()
            value_copy(h).wait_recv()
            first = (kbuf[:, cols(h)], vbuf[:, cols(h)])
            second = (k_ref[:, cols(h)], v_ref[:, cols(h)])
            early = dot_tn(first[1], first[0])
            s_send[h] = (early + dot_tn(second[1], second[0])).astype(BF16)
            state_copy(h, 0, 0, 2).start()
            query_copy(h, 0, 1).wait_recv()
            emit(h, 0, *part(qbuf[0, :, cols(h)], (first, second)))
            for copy in part_copies(h, 0, 0, 2):
                copy.start()
            query = q_ref[:, cols(h)]
            windowed = merged(h, [part(query, (first,)) + (False,)])
            finish(h, windowed, lin[h] + dot_nt(early.astype(BF16), query))
            relay_copy(h).wait_recv()
            emit(h, 1, *part(qbuf[1, :, cols(h)], (first, second)))
            for copy in part_copies(h, 1, 0, 3):
                copy.start()

        def drain(h):
            state_copy(h, 0, 0, 2).wait_send()
            for copy in part_copies(h, 0, 0, 2) + part_copies(h, 1, 0, 3):
                copy.wait_send()

        loop(own)
        loop(work)
        loop(drain)

    @pl.when(seq == 2)
    def _():
        def first(h):
            query_copy(h, 0, 1).start()
            own(h)
            key, value = k_ref[:, cols(h)], v_ref[:, cols(h)]
            s_send[h] = dot_tn(value, key).astype(BF16)
            state_copy(h, 0, 1, 3).start()
            query_copy(h, 1, 2).wait_recv()
            relay_copy(h).start()
            emit(h, 1, *part(qbuf[1, :, cols(h)], ((key, value),)))
            for copy in part_copies(h, 1, 1, 3):
                copy.start()

        def second(h):
            project_before(h)
            state_copy(h, 0, 0, 2).wait_recv()
            prefix_copy(h).start()
            for copy in part_copies(h, 0, 0, 2):
                copy.wait_recv()
            linear = lin[h] + dot_nt(s_recv[0, h], q_ref[:, cols(h)])
            finish(h, merged(h, [received(h, 0)]), linear)

        def drain(h):
            query_copy(h, 0, 1).wait_send()
            relay_copy(h).wait_send()
            state_copy(h, 0, 1, 3).wait_send()
            prefix_copy(h).wait_send()
            for copy in part_copies(h, 1, 1, 3):
                copy.wait_send()

        loop(first)
        loop(second)
        loop(drain)

    @pl.when(seq == 3)
    def _():
        def send(h):
            query_copy(h, 1, 2).start()

        def work(h):
            project_before(h)
            state_copy(h, 0, 1, 3).wait_recv()
            prefix_copy(h).wait_recv()
            for copy in part_copies(h, 1, 1, 3) + part_copies(h, 1, 0, 3):
                copy.wait_recv()
            query = q_ref[:, cols(h)]
            linear = lin[h] + dot_nt(s_recv[0, h], query) + dot_nt(s_recv[1, h], query)
            finish(h, merged(h, [received(h, 0), received(h, 1)]), linear)

        def drain(h):
            query_copy(h, 1, 2).wait_send()

        loop(send)
        loop(own)
        loop(work)
        loop(drain)

    project(heads - 1)
    out_ref[...] = summed[...].astype(BF16)


def fused(queries, keys, values, w_out):
    peers = lax.axis_size("head")
    length, width = queries.shape
    heads = width // HD
    share = length // peers
    dma = pltpu.SemaphoreType.DMA
    vmem = pl.BlockSpec(memory_space=pltpu.VMEM)
    return pl.pallas_call(
        functools.partial(kernel, peers),
        out_shape=jax.ShapeDtypeStruct((share, w_out.shape[1]), BF16),
        in_specs=[pl.BlockSpec(memory_space=pltpu.HBM)] * 4,
        out_specs=vmem,
        scratch_shapes=[
            pltpu.VMEM((length, width), BF16),
            pltpu.VMEM((length, width), BF16),
            pltpu.VMEM((length, width), BF16),
            pltpu.VMEM((heads, peers * HD, w_out.shape[1]), BF16),
            pltpu.VMEM((share, w_out.shape[1]), F32),
            pltpu.VMEM((length, width), BF16),
            pltpu.VMEM((length, width), BF16),
            pltpu.VMEM((2, length, width), BF16),
            pltpu.VMEM((2, heads, HD, length), BF16),
            pltpu.VMEM((2, heads, HD, length), BF16),
            pltpu.VMEM((2, heads, 2, length), F32),
            pltpu.VMEM((2, heads, 2, length), F32),
            pltpu.VMEM((heads, HD, HD), BF16),
            pltpu.VMEM((2, heads, HD, HD), BF16),
            pltpu.VMEM((heads, HD, length), F32),
            pltpu.VMEM((heads, HD, length), F32),
            pltpu.VMEM((heads, 8, length), F32),
            pltpu.VMEM((width, length), BF16),
            pltpu.VMEM((heads, peers * HD, share), BF16),
            dma((3,)), dma((heads, peers)), dma((2, heads)), dma((2, heads)), dma((2, heads)), dma((2, heads)),
            dma((2, heads)), dma((2, heads)), dma((2, heads)), dma((2, heads)),
            dma((2, heads)), dma((2, heads)), dma((heads, peers)), dma((heads, peers)),
        ],
        compiler_params=pltpu.CompilerParams(
            collective_id=0, has_side_effects=True, vmem_limit_bytes=56 * 1024 * 1024
        ),
    )(queries, keys, values, w_out)


def shifted(value, axis, steps):
    count = lax.axis_size(axis)
    first, last = (max(0, -steps), min(count, count - steps))
    return lax.ppermute(value, axis, [(source, source + steps) for source in range(first, last)])


def fits(queries):
    length, width = queries.shape
    blocks = lax.axis_size("seq")
    share = length // lax.axis_size("head")
    return blocks == 4 and blocks * length <= WINDOW and share % HD == 0 and width % HD == 0


def per_device(queries, keys, values, w_out):
    if fits(queries):
        return fused(queries, keys, values, w_out)
    length_dev, width = queries.shape
    heads_dev = width // HD
    block_rows = min(512, length_dev)
    block_count = length_dev // block_rows
    highest = lax.Precision.HIGHEST
    seq_index = lax.axis_index("seq")
    q_blocks = queries.reshape(block_count, block_rows, heads_dev, HD)
    k_blocks = keys.reshape(block_count, block_rows, heads_dev, HD)
    v_blocks = values.reshape(block_count, block_rows, heads_dev, HD)
    block_states = jnp.einsum(
        "bkhd,bkhe->bhde", k_blocks, v_blocks, preferred_element_type=jnp.float32
    )
    own_state = jnp.sum(block_states, axis=0)
    earlier = jnp.cumsum(block_states, axis=0) - block_states
    piece = lax.all_gather(own_state[None], "seq", axis=0, tiled=True)
    order = jnp.arange(piece.shape[0], dtype=jnp.int32)
    keep = order < seq_index
    prefix = jnp.sum(jnp.where(keep[:, None, None, None], piece, 0.0), axis=0)
    causal = jnp.arange(block_rows)[:, None] >= jnp.arange(block_rows)[None, :]
    local_scores = jnp.einsum(
        "bqhd,bkhd->bhqk", q_blocks, k_blocks, preferred_element_type=jnp.float32
    )
    local_scores = jnp.where(causal, local_scores, 0.0)
    intra = jnp.einsum(
        "bhqk,bkhe->bqhe", local_scores, v_blocks.astype(jnp.float32), precision=highest
    )
    state_before = prefix[None] + earlier
    inter = jnp.einsum(
        "bqhd,bhde->bqhe", q_blocks.astype(jnp.float32), state_before, precision=highest
    )
    linear = (intra + inter).reshape(length_dev, heads_dev, HD)
    normed = linear / jnp.sqrt(jnp.mean(linear * linear, axis=-1, keepdims=True) + 1e-06)
    reach = min(WINDOW // length_dev, lax.axis_size("seq") - 1)
    received = [shifted((keys, values), "seq", distance) for distance in range(1, reach + 1)]
    pad_rows = WINDOW - reach * length_dev
    filler = jnp.zeros((pad_rows, width), keys.dtype)
    wide_keys = jnp.concatenate([filler] + [pair[0] for pair in reversed(received)] + [keys], 0)
    wide_values = jnp.concatenate([filler] + [pair[1] for pair in reversed(received)] + [values], 0)
    wide_keys = wide_keys.reshape(-1, heads_dev, HD)
    wide_values = wide_values.reshape(-1, heads_dev, HD)
    scale = 1.0 / math.sqrt(HD)
    span = WINDOW + block_rows
    query_pos = jnp.arange(block_rows, dtype=jnp.int32)[:, None]
    key_pos = jnp.arange(span, dtype=jnp.int32)[None, :]
    band = (key_pos > query_pos) & (key_pos <= query_pos + WINDOW)
    rows_q = queries.reshape(block_rows, heads_dev, HD)
    anchor = seq_index * length_dev + 0 - WINDOW
    valid = band & (anchor + key_pos >= 0)
    scores = (
        jnp.einsum("qhd,khd->hqk", rows_q, wide_keys, preferred_element_type=jnp.float32) * scale
    )
    scores = jnp.where(valid[None], scores, -1e30)
    top = jnp.max(scores, axis=-1, keepdims=True)
    expo = jnp.where(valid[None], jnp.exp(scores - top), 0.0)
    total = jnp.sum(expo, axis=-1)
    weights = expo.astype(jnp.bfloat16)
    summed = jnp.einsum("hqk,khe->qhe", weights, wide_values, preferred_element_type=jnp.float32)
    pieces = summed / jnp.transpose(total)[:, :, None]
    mixed = (normed + pieces).astype(jnp.bfloat16).reshape(length_dev, width)
    head_count = lax.axis_size("head")
    share = length_dev // head_count
    grouped = mixed.reshape(head_count, share, width)
    return jnp.dot(
        lax.all_to_all(grouped, "head", split_axis=0, concat_axis=2, tiled=True)[0],
        w_out,
        preferred_element_type=jnp.float32,
    ).astype(jnp.bfloat16)


def solution(mesh):
    return jax.shard_map(
        per_device,
        mesh=mesh,
        in_specs=(
            P(("groups", "seq"), "head"),
            P(("groups", "seq"), "head"),
            P(("groups", "seq"), "head"),
            P(),
        ),
        out_specs=P(("groups", "seq", "head"), None),
        check_vma=False,
    )
```

profile of v0, /device:TPU:25, one launch (start us, length us, event | category | flops | bytes accessed | tf_op | source)
XLA Modules:
  0.0 51.6 jit_solution(4858589241006081204)
XLA Ops:
  0.0 49.7 %shard_map.46 = bf16[128,2048]{1,0:T(8,128)(2,1)} custom-call(bf16[512,512]{1,0:T(8,128)(2,1)} %q_hbm.1, bf16[512,512]{1,0:T(8,128)(2,1)} %k_hbm.1, bf16[512,512]{1,0:T(8,128)(2,1)} %v_hbm.1, bf16[2048,2048]{1,0:T(8,128)(2,1)} %w_hbm.1), custom_call_target="tpu_custom_call" | custom-call | tf_op jit(solution)/shard_map/pallas_call | solution.py:336
  49.7 1.9 %copy.6 = bf16[128,2048]{1,0:T(8,128)(2,1)} copy(bf16[128,2048]{1,0:T(8,128)(2,1)} %shard_map.46) | data formatting | bytes 1048576
where the time goes:
time: 51.7 us; the launch traced here: 51.6 us
  Pallas kernels  49.7 us (96%)
  local copies, waits for them, and re-layouts  1.88 us (4%)
    pallas_call x1, Pallas kernels, fused(): pl.pallas_call(functools.partial(kernel, peers), out_shape=jax.ShapeDtype...  49.7 us
    unnamed x1, local copies, waits for them, and re-layouts  1.88 us

commit v1 on v0

v1 whole, which is shorter than its diff:
```python
import functools
import math

import jax
import jax.numpy as jnp
from jax import lax
from jax.experimental import pallas as pl
from jax.experimental.pallas import tpu as pltpu
from jax.sharding import PartitionSpec as P

HD = 128
WINDOW = 2048
MESH = pl.DeviceIdType.MESH
F32 = jnp.float32
BF16 = jnp.bfloat16
RATE = math.log2(math.e) / math.sqrt(HD)
FLOOR = -1e30


def dot_nt(a, b):
    return lax.dot_general(a, b, (((1,), (1,)), ((), ())), preferred_element_type=F32)


def dot_tn(a, b):
    return lax.dot_general(a, b, (((0,), (0,)), ((), ())), preferred_element_type=F32)


def recip(x):
    return 1.0 / x


def lanes(index, size):
    return pl.ds(pl.multiple_of(index * size, size), size)


def kernel(
    peers, q_hbm, k_hbm, v_hbm, w_hbm, out_ref, q_ref, k_ref, v_ref,
    w_ref, summed, kbuf, vbuf, qbuf, ebuf, pacc, pstat, o_send, o_recv, o_part, l_send, l_recv, l_part,
    s_send, s_recv, acc, lin, stat, mixed, gathered,
    in_sem, w_sem, kv_tx, kv_rx, q_tx, q_rx, o_tx, o_rx, l_tx, l_rx, p_tx, p_rx, s_tx, s_rx, m_tx, m_rx, turn,
):
    seq = lax.axis_index("seq")
    here = lax.axis_index("head")
    length, width = q_ref.shape
    heads = width // HD
    share = length // peers
    chip, core = here // 2, here % 2
    chips = peers // 2
    order = list(range(2, peers)) + [1, 0]

    def peer_of(index, sign=1):
        hop, flip = index // 2, index % 2
        other = lax.rem(chip + sign * hop + chips, chips)
        return other * 2 + (1 - core if flip else core)

    barrier = pltpu.get_barrier_semaphore()

    def greet(device):
        pl.semaphore_signal(barrier, inc=1, device_id=device, device_id_type=MESH)

    for index in range(1, peers):
        greet({"head": peer_of(index)})
    circle = {0: (1,), 1: (0, 2, 3), 2: (1, 3), 3: (1, 2)}
    for place, friends in circle.items():
        @pl.when(seq == place)
        def _():
            for friend in friends:
                greet({"seq": friend})

    loads = [
        pltpu.make_async_copy(source, target, in_sem.at[i])
        for i, (source, target) in enumerate(((q_hbm, q_ref), (k_hbm, k_ref), (v_hbm, v_ref)))
    ]
    for load in loads:
        load.start()

    def load_w(h, peer):
        return pltpu.make_async_copy(
            w_hbm.at[pl.ds(pl.multiple_of(peer * width + h * HD, HD), HD), :],
            w_ref.at[h, pl.ds(peer * HD, HD), :],
            w_sem.at[h, peer],
        )

    def load_head(h):
        for peer in range(peers):
            load_w(h, peer).start()

    for place, friends in circle.items():
        @pl.when(seq == place)
        def _():
            pl.semaphore_wait(barrier, len(friends) + peers - 1)
    for load in loads:
        load.wait()

    def cols(h):
        return lanes(h, HD)

    def remote(source, target, tx, rx, device):
        return pltpu.make_async_remote_copy(
            src_ref=source, dst_ref=target, send_sem=tx, recv_sem=rx,
            device_id=device, device_id_type=MESH,
        )

    def kv_copies(h):
        return [
            remote(
                source.at[:, cols(h)], target.at[:, cols(h)], kv_tx.at[i, h], kv_rx.at[i, h], {"seq": 1}
            )
            for i, (source, target) in enumerate(((k_ref, kbuf), (v_ref, vbuf)))
        ]

    def near_copies():
        return [
            remote(
                source.at[:, cols(0)], target.at[:, cols(1)], kv_tx.at[i, 1], kv_rx.at[i, 1], {"seq": 2}
            )
            for i, (source, target) in enumerate(((k_ref, kbuf), (v_ref, vbuf)))
        ]

    def far_copies():
        return [
            remote(
                buffer.at[:, cols(0)], buffer.at[:, cols(0)], kv_tx.at[i, 0], kv_rx.at[i, 0], {"seq": 2}
            )
            for i, buffer in enumerate((kbuf, vbuf))
        ]

    def query_copy(h, slot, target):
        return remote(
            q_ref.at[:, cols(h)], qbuf.at[slot, :, cols(h)],
            q_tx.at[slot, h], q_rx.at[slot, h], {"seq": target},
        )

    def relay_copy(h):
        return remote(
            qbuf.at[1, :, cols(h)], qbuf.at[1, :, cols(h)], q_tx.at[1, h], q_rx.at[1, h], {"seq": 1}
        )

    def level_copy(h, slot):
        return remote(
            l_send.at[slot, h], l_recv.at[h], l_tx.at[slot, h], l_rx.at[h], {"seq": 2 + slot}
        )

    def chunk_copy(h, slot, index):
        place = lanes(peer_of(index), share)
        return remote(
            o_send.at[slot, h, :, place], o_recv.at[h, :, place],
            o_tx.at[slot, h, index], o_rx.at[h, index], {"seq": 2 + slot},
        )

    def part_copies(h):
        return (
            remote(l_send.at[1, h], l_part.at[h], p_tx.at[0, h], p_rx.at[0, h], {"seq": 3}),
            remote(o_send.at[1, h], o_part.at[h], p_tx.at[1, h], p_rx.at[1, h], {"seq": 3}),
        )

    def state_copy(h, tx_slot, in_slot, target):
        return remote(
            s_send.at[h], s_recv.at[in_slot, h], s_tx.at[tx_slot, h], s_rx.at[in_slot, h],
            {"seq": target},
        )

    def prefix_copy(h):
        return remote(
            s_recv.at[0, h], s_recv.at[0, h], s_tx.at[1, h], s_rx.at[0, h], {"seq": 3}
        )

    def mixed_copy(h, index):
        target = peer_of(index)
        return remote(
            mixed.at[cols(h), lanes(target, share)], gathered.at[h, lanes(here, HD), :],
            m_tx.at[h, index], m_rx.at[h, index], {"head": target},
        )

    def loop(body, first=0):
        lax.fori_loop(first, heads, lambda h, c: (body(h), c)[1], 0)

    causal = lax.broadcasted_iota(jnp.int32, (length, length), 0) <= lax.broadcasted_iota(
        jnp.int32, (length, length), 1
    )

    def level(top, total):
        return top * RATE + jnp.log2(total)

    def own(h):
        query, key, value = q_ref[:, cols(h)], k_ref[:, cols(h)], v_ref[:, cols(h)]
        scores = dot_nt(key, query)
        kept = jnp.where(causal, scores, 0.0)
        coarse = kept.astype(BF16)
        fine = (kept - coarse.astype(F32)).astype(BF16)
        lin[h] = dot_tn(value, coarse) + dot_tn(value, fine)
        scores = jnp.where(causal, scores, FLOOR)
        top = jnp.max(scores, axis=0, keepdims=True)
        expo = jnp.exp2((scores - top) * RATE)
        total = jnp.sum(expo, axis=0, keepdims=True)
        stat[h, 0:1, :] = level(top, total)
        acc[h] = dot_tn(value, expo.astype(BF16)) * recip(total)

    def part(query, pairs):
        scores = [dot_nt(key, query) for key, _ in pairs]
        top = functools.reduce(jnp.maximum, [jnp.max(s, axis=0, keepdims=True) for s in scores])
        expo = [jnp.exp2((s - top) * RATE) for s in scores]
        total = sum(jnp.sum(e, axis=0, keepdims=True) for e in expo)
        output = sum(dot_tn(value, e.astype(BF16)) for e, (_, value) in zip(expo, pairs))
        return level(top, total), output * recip(total)

    def blend(a, b):
        top = jnp.maximum(a[0], b[0])
        left, right = jnp.exp2(a[0] - top), jnp.exp2(b[0] - top)
        total = left + right
        scale = recip(total)
        return top + jnp.log2(total), (left * scale) * a[1] + (right * scale) * b[1]

    def current(h):
        return stat[h, 0:1, :], acc[h]

    def norm(linear):
        square = jnp.mean(linear * linear, axis=0, keepdims=True)
        return linear * recip(jnp.sqrt(square + 1e-06))

    def finish(h, windowed, linear):
        mixed[cols(h), :] = (norm(linear) + windowed).astype(BF16)
        for index in order[:-1]:
            mixed_copy(h, index).start()
        gathered[h, lanes(here, HD), :] = mixed[cols(h), lanes(here, share)]

    def arrive(h):
        level_copy(h, 0).wait_recv()
        for index in order:
            chunk_copy(h, 0, index).wait_recv()
            place = lanes(peer_of(index), share)
            mine = stat[h, 0:1, place], acc[h, :, place]
            theirs = l_recv[h, 0:1, place], o_recv[h, :, place].astype(F32)
            piece = (lin[h, :, place] + blend(mine, theirs)[1]).astype(BF16)
            if index:
                mixed[cols(h), place] = piece
                mixed_copy(h, index).start()
            else:
                gathered[h, lanes(here, HD), :] = piece

    tile = math.gcd(w_ref.shape[2], 512)

    def project(h):
        for peer in range(peers):
            load_w(h, peer).wait()
        for index in range(1, peers):
            mixed_copy(h, index).wait()
        left = gathered[h].T

        @pl.loop(0, w_ref.shape[2] // tile)
        def _(index):
            part_cols = lanes(index, tile)
            summed[:, part_cols] += jnp.dot(
                left, w_ref[h, :, part_cols], preferred_element_type=F32
            )

    def project_before(h):
        @pl.when(h > 0)
        def _():
            project(h - 1)

    def weights():
        lax.fori_loop(0, heads, lambda h, c: (load_head(h), c)[1], 0)
        summed[...] = jnp.zeros_like(summed)

    @pl.when(seq == 0)
    def _():
        def send(h):
            for copy in kv_copies(h):
                copy.start()

        def work(h):
            own(h)
            finish(h, acc[h], lin[h])
            project_before(h)

        def drain(h):
            kv_copies(h)[1].wait_send()

            @pl.when(h > 0)
            def _():
                kv_copies(h)[0].wait_send()

        @pl.when(core == 0)
        def _():
            loop(send)
            kv_copies(0)[0].wait_send()
            pl.semaphore_signal(
                turn, inc=1, device_id={"head": peer_of(1)}, device_id_type=MESH
            )

        weights()

        @pl.when(core == 1)
        def _():
            pl.semaphore_wait(turn, 1)
            loop(send)
            kv_copies(0)[0].wait_send()

        loop(work)
        loop(drain)

    @pl.when(seq == 1)
    def _():
        for copy in near_copies():
            copy.start()
        weights()
        loop(own)

        def pre(h):
            for slot in range(2):
                query_copy(h, slot, 1).wait_recv()
                bottom, output = part(
                    qbuf[slot, :, cols(h)], ((k_ref[:, cols(h)], v_ref[:, cols(h)]),)
                )
                pstat[slot, 0:1, :] = bottom
                pacc[slot] = output

        def rest(h, early):
            query = q_ref[:, cols(h)]
            windowed = blend(current(h), part(query, ((kbuf[:, cols(h)], vbuf[:, cols(h)]),)))[1]
            finish(h, windowed, lin[h] + dot_nt(early, query))

        def early_state(h):
            return dot_tn(vbuf[:, cols(h)], kbuf[:, cols(h)])

        for arrived, onward in zip(kv_copies(0), far_copies()):
            arrived.wait_recv()
            onward.start()
        rest(0, early_state(0).astype(BF16))
        pre(1)

        def work(h):
            arrived = kv_copies(h)
            arrived[0].wait_recv()
            for slot in range(2):
                scores = dot_nt(kbuf[:, cols(h)], qbuf[slot, :, cols(h)])
                top = jnp.max(scores, axis=0, keepdims=True)
                expo = jnp.exp2((scores - top) * RATE)
                total = jnp.sum(expo, axis=0, keepdims=True)
                pstat[slot, 1:2, :] = level(top, total)
                pstat[slot, 2:3, :] = recip(total)
                ebuf[slot] = expo.astype(BF16)
            arrived[1].wait_recv()
            early = early_state(h)
            s_send[h] = (early + dot_tn(v_ref[:, cols(h)], k_ref[:, cols(h)])).astype(BF16)
            state_copy(h, 0, 0, 2).start()
            for slot in (1, 0):
                fresh = dot_tn(vbuf[:, cols(h)], ebuf[slot]) * pstat[slot, 2:3, :]
                bottom, output = blend(
                    (pstat[slot, 0:1, :], pacc[slot]), (pstat[slot, 1:2, :], fresh)
                )
                l_send[slot, h] = bottom
                o_send[slot, h] = output.astype(BF16)
                level_copy(h, slot).start()
                for index in order:
                    chunk_copy(h, slot, index).start()

            @pl.when(h + 1 < heads)
            def _():
                pre(h + 1)

            rest(h, early.astype(BF16))
            project(h - 1)

        def drain(h):
            state_copy(h, 0, 0, 2).wait_send()
            for slot in range(2):
                level_copy(h, slot).wait_send()
                for index in order:
                    chunk_copy(h, slot, index).wait_send()

        loop(work, 1)
        for copy in near_copies() + far_copies():
            copy.wait_send()
        loop(drain, 1)

    @pl.when(seq == 2)
    def _():
        loop(lambda h: query_copy(h, 0, 1).start(), 1)
        weights()

        def first(h):
            own(h)
            s_send[h] = dot_tn(v_ref[:, cols(h)], k_ref[:, cols(h)]).astype(BF16)
            state_copy(h, 0, 1, 3).start()

        def emit(h, pairs):
            bottom, output = part(qbuf[1, :, cols(h)], pairs)
            l_send[1, h] = bottom
            o_send[1, h] = output.astype(BF16)
            for copy in part_copies(h):
                copy.start()

        def middle(h):
            query_copy(h, 1, 2).wait_recv()
            relay_copy(h).start()
            emit(h, ((k_ref[:, cols(h)], v_ref[:, cols(h)]),))

        loop(first)
        loop(middle, 1)
        query_copy(0, 1, 2).wait_recv()
        for copy in near_copies() + far_copies():
            copy.wait_recv()
        pairs = [(kbuf[:, cols(i)], vbuf[:, cols(i)]) for i in range(2)]
        s_recv[0, 0] = sum(dot_tn(value, key) for key, value in pairs).astype(BF16)
        prefix_copy(0).start()
        emit(0, pairs + [(k_ref[:, cols(0)], v_ref[:, cols(0)])])
        query = q_ref[:, cols(0)]
        windowed = blend(current(0), part(query, pairs))[1]
        finish(0, windowed, lin[0] + dot_nt(s_recv[0, 0], query))

        def second(h):
            state_copy(h, 0, 0, 2).wait_recv()
            prefix_copy(h).start()
            lin[h] = norm(lin[h] + dot_nt(s_recv[0, h], q_ref[:, cols(h)]))
            arrive(h)
            project(h - 1)

        def drain(h):
            @pl.when(h > 0)
            def _():
                query_copy(h, 0, 1).wait_send()
                relay_copy(h).wait_send()

            state_copy(h, 0, 1, 3).wait_send()
            prefix_copy(h).wait_send()
            for copy in part_copies(h):
                copy.wait_send()

        loop(second, 1)
        loop(drain)

    @pl.when(seq == 3)
    def _():
        for h in [1, 0] + list(range(2, heads)):
            query_copy(h, 1, 2).start()
        weights()
        loop(own)

        def join(h):
            for copy in part_copies(h):
                copy.wait_recv()
            bottom, output = blend(current(h), (l_part[h], o_part[h].astype(F32)))
            stat[h, 0:1, :] = bottom
            acc[h] = output
            state_copy(h, 0, 1, 3).wait_recv()
            lin[h] += dot_nt(s_recv[1, h], q_ref[:, cols(h)])

        def linear(h):
            prefix_copy(h).wait_recv()
            return lin[h] + dot_nt(s_recv[0, h], q_ref[:, cols(h)])

        loop(join, 1)
        join(0)
        finish(0, acc[0], linear(0))

        def work(h):
            lin[h] = norm(linear(h))
            arrive(h)
            project(h - 1)

        loop(work, 1)
        loop(lambda h: query_copy(h, 1, 2).wait_send())

    project(heads - 1)
    out_ref[...] = summed[...].astype(BF16)


def fused(queries, keys, values, w_out):
    peers = lax.axis_size("head")
    length, width = queries.shape
    heads = width // HD
    share = length // peers
    dma = pltpu.SemaphoreType.DMA
    vmem = pl.BlockSpec(memory_space=pltpu.VMEM)
    return pl.pallas_call(
        functools.partial(kernel, peers),
        out_shape=jax.ShapeDtypeStruct((share, w_out.shape[1]), BF16),
        in_specs=[pl.BlockSpec(memory_space=pltpu.HBM)] * 4,
        out_specs=vmem,
        scratch_shapes=[
            pltpu.VMEM((length, width), BF16),
            pltpu.VMEM((length, width), BF16),
            pltpu.VMEM((length, width), BF16),
            pltpu.VMEM((heads, peers * HD, w_out.shape[1]), BF16),
            pltpu.VMEM((share, w_out.shape[1]), F32),
            pltpu.VMEM((length, width), BF16),
            pltpu.VMEM((length, width), BF16),
            pltpu.VMEM((2, length, width), BF16),
            pltpu.VMEM((2, length, length), BF16),
            pltpu.VMEM((2, HD, length), F32),
            pltpu.VMEM((2, 8, length), F32),
            pltpu.VMEM((2, heads, HD, length), BF16),
            pltpu.VMEM((heads, HD, length), BF16),
            pltpu.VMEM((heads, HD, length), BF16),
            pltpu.VMEM((2, heads, 1, length), F32),
            pltpu.VMEM((heads, 1, length), F32),
            pltpu.VMEM((heads, 1, length), F32),
            pltpu.VMEM((heads, HD, HD), BF16),
            pltpu.VMEM((2, heads, HD, HD), BF16),
            pltpu.VMEM((heads, HD, length), F32),
            pltpu.VMEM((heads, HD, length), F32),
            pltpu.VMEM((heads, 8, length), F32),
            pltpu.VMEM((width, length), BF16),
            pltpu.VMEM((heads, peers * HD, share), BF16),
            dma((3,)), dma((heads, peers)), dma((2, heads)), dma((2, heads)), dma((2, heads)), dma((2, heads)),
            dma((2, heads, peers)), dma((heads, peers)), dma((2, heads)), dma((heads,)), dma((2, heads)), dma((2, heads)),
            dma((2, heads)), dma((2, heads)), dma((heads, peers)), dma((heads, peers)),
            pltpu.SemaphoreType.REGULAR,
        ],
        compiler_params=pltpu.CompilerParams(
            collective_id=0, has_side_effects=True, vmem_limit_bytes=56 * 1024 * 1024
        ),
    )(queries, keys, values, w_out)


def shifted(value, axis, steps):
    count = lax.axis_size(axis)
    first, last = (max(0, -steps), min(count, count - steps))
    return lax.ppermute(value, axis, [(source, source + steps) for source in range(first, last)])


def fits(queries):
    length, width = queries.shape
    blocks = lax.axis_size("seq")
    share = length // lax.axis_size("head")
    whole = share % HD == 0 and width % HD == 0 and width > HD and lax.axis_size("head") % 2 == 0
    return blocks == 4 and blocks * length <= WINDOW and whole


def per_device(queries, keys, values, w_out):
    if fits(queries):
        return fused(queries, keys, values, w_out)
    length_dev, width = queries.shape
    heads_dev = width // HD
    block_rows = min(512, length_dev)
    block_count = length_dev // block_rows
    highest = lax.Precision.HIGHEST
    seq_index = lax.axis_index("seq")
    q_blocks = queries.reshape(block_count, block_rows, heads_dev, HD)
    k_blocks = keys.reshape(block_count, block_rows, heads_dev, HD)
    v_blocks = values.reshape(block_count, block_rows, heads_dev, HD)
    block_states = jnp.einsum(
        "bkhd,bkhe->bhde", k_blocks, v_blocks, preferred_element_type=jnp.float32
    )
    own_state = jnp.sum(block_states, axis=0)
    earlier = jnp.cumsum(block_states, axis=0) - block_states
    piece = lax.all_gather(own_state[None], "seq", axis=0, tiled=True)
    order = jnp.arange(piece.shape[0], dtype=jnp.int32)
    keep = order < seq_index
    prefix = jnp.sum(jnp.where(keep[:, None, None, None], piece, 0.0), axis=0)
    causal = jnp.arange(block_rows)[:, None] >= jnp.arange(block_rows)[None, :]
    local_scores = jnp.einsum(
        "bqhd,bkhd->bhqk", q_blocks, k_blocks, preferred_element_type=jnp.float32
    )
    local_scores = jnp.where(causal, local_scores, 0.0)
    intra = jnp.einsum(
        "bhqk,bkhe->bqhe", local_scores, v_blocks.astype(jnp.float32), precision=highest
    )
    state_before = prefix[None] + earlier
    inter = jnp.einsum(
        "bqhd,bhde->bqhe", q_blocks.astype(jnp.float32), state_before, precision=highest
    )
    linear = (intra + inter).reshape(length_dev, heads_dev, HD)
    normed = linear / jnp.sqrt(jnp.mean(linear * linear, axis=-1, keepdims=True) + 1e-06)
    reach = min(WINDOW // length_dev, lax.axis_size("seq") - 1)
    received = [shifted((keys, values), "seq", distance) for distance in range(1, reach + 1)]
    pad_rows = WINDOW - reach * length_dev
    filler = jnp.zeros((pad_rows, width), keys.dtype)
    wide_keys = jnp.concatenate([filler] + [pair[0] for pair in reversed(received)] + [keys], 0)
    wide_values = jnp.concatenate([filler] + [pair[1] for pair in reversed(received)] + [values], 0)
    wide_keys = wide_keys.reshape(-1, heads_dev, HD)
    wide_values = wide_values.reshape(-1, heads_dev, HD)
    scale = 1.0 / math.sqrt(HD)
    span = WINDOW + block_rows
    query_pos = jnp.arange(block_rows, dtype=jnp.int32)[:, None]
    key_pos = jnp.arange(span, dtype=jnp.int32)[None, :]
    band = (key_pos > query_pos) & (key_pos <= query_pos + WINDOW)
    rows_q = queries.reshape(block_rows, heads_dev, HD)
    anchor = seq_index * length_dev + 0 - WINDOW
    valid = band & (anchor + key_pos >= 0)
    scores = (
        jnp.einsum("qhd,khd->hqk", rows_q, wide_keys, preferred_element_type=jnp.float32) * scale
    )
    scores = jnp.where(valid[None], scores, -1e30)
    top = jnp.max(scores, axis=-1, keepdims=True)
    expo = jnp.where(valid[None], jnp.exp(scores - top), 0.0)
    total = jnp.sum(expo, axis=-1)
    weights = expo.astype(jnp.bfloat16)
    summed = jnp.einsum("hqk,khe->qhe", weights, wide_values, preferred_element_type=jnp.float32)
    pieces = summed / jnp.transpose(total)[:, :, None]
    mixed = (normed + pieces).astype(jnp.bfloat16).reshape(length_dev, width)
    head_count = lax.axis_size("head")
    share = length_dev // head_count
    grouped = mixed.reshape(head_count, share, width)
    return jnp.dot(
        lax.all_to_all(grouped, "head", split_axis=0, concat_axis=2, tiled=True)[0],
        w_out,
        preferred_element_type=jnp.float32,
    ).astype(jnp.bfloat16)


def solution(mesh):
    return jax.shard_map(
        per_device,
        mesh=mesh,
        in_specs=(
            P(("groups", "seq"), "head"),
            P(("groups", "seq"), "head"),
            P(("groups", "seq"), "head"),
            P(),
        ),
        out_specs=P(("groups", "seq", "head"), None),
        check_vma=False,
    )
```

time: 51.7 us -> 46.3 us (0.90); the launches traced: 51.6 us -> 45.5 us
  Pallas kernels: 49.7 us -> 43.6 us
    pallas_call x1, Pallas kernels: 49.7 us -> 43.6 us  [fused(): pl.pallas_call(functools.partial(kernel, peers), out_shape=jax.ShapeDtype...]
where the time goes in v1:
time: 46.3 us; the launch traced here: 45.5 us
  Pallas kernels  43.6 us (94%)
  local copies, waits for them, and re-layouts  1.88 us (4%)
    pallas_call x1, Pallas kernels, fused(): pl.pallas_call(functools.partial(kernel, peers), out_shape=jax.ShapeDtype...  43.6 us
    unnamed x1, local copies, waits for them, and re-layouts  1.88 us

profile of v1, /device:TPU:25, one launch (start us, length us, event | category | flops | bytes accessed | tf_op | source)
XLA Modules:
  0.0 45.5 jit_solution(15914215160819845773)
XLA Ops:
  0.0 43.6 %shard_map.46 = bf16[128,2048]{1,0:T(8,128)(2,1)} custom-call(bf16[512,512]{1,0:T(8,128)(2,1)} %q_hbm.1, bf16[512,512]{1,0:T(8,128)(2,1)} %k_hbm.1, bf16[512,512]{1,0:T(8,128)(2,1)} %v_hbm.1, bf16[2048,2048]{1,0:T(8,128)(2,1)} %w_hbm.1), custom_call_target="tpu_custom_call" | custom-call | tf_op jit(solution)/shard_map/pallas_call | solution.py:477
  43.6 1.9 %copy.6 = bf16[128,2048]{1,0:T(8,128)(2,1)} copy(bf16[128,2048]{1,0:T(8,128)(2,1)} %shard_map.46) | data formatting | bytes 1048576

commit v2 on v1

--- a/solution.py
+++ b/solution.py
@@ -37,7 +37,7 @@
     peers, q_hbm, k_hbm, v_hbm, w_hbm, out_ref, q_ref, k_ref, v_ref,
     w_ref, summed, kbuf, vbuf, qbuf, ebuf, pacc, pstat, o_send, o_recv, o_part, l_send, l_recv, l_part,
     s_send, s_recv, acc, lin, stat, mixed, gathered,
-    in_sem, w_sem, kv_tx, kv_rx, q_tx, q_rx, o_tx, o_rx, l_tx, l_rx, p_tx, p_rx, s_tx, s_rx, m_tx, m_rx, turn,
+    in_sem, w_sem, tx, kv_rx, q_rx, o_rx, l_rx, s_rx, m_rx,
 ):
     seq = lax.axis_index("seq")
     here = lax.axis_index("head")
@@ -78,7 +78,7 @@
         return pltpu.make_async_copy(
             w_hbm.at[pl.ds(pl.multiple_of(peer * width + h * HD, HD), HD), :],
             w_ref.at[h, pl.ds(peer * HD, HD), :],
-            w_sem.at[h, peer],
+            w_sem.at[h],
         )
 
     def load_head(h):
@@ -95,85 +95,84 @@
     def cols(h):
         return lanes(h, HD)
 
-    def remote(source, target, tx, rx, device):
+    def remote(source, target, sent, landed, device):
         return pltpu.make_async_remote_copy(
-            src_ref=source, dst_ref=target, send_sem=tx, recv_sem=rx,
+            src_ref=source, dst_ref=target, send_sem=tx.at[sent], recv_sem=landed,
             device_id=device, device_id_type=MESH,
         )
 
-    def kv_copies(h):
+    def settle(ref, semaphore):
+        pltpu.make_async_copy(ref, ref, semaphore).wait()
+
+    def kv_copies(h, target=1, first=0):
         return [
             remote(
-                source.at[:, cols(h)], target.at[:, cols(h)], kv_tx.at[i, h], kv_rx.at[i, h], {"seq": 1}
+                source.at[:, cols(h)], buffer.at[:, cols(h)], first + i, kv_rx.at[i, h], {"seq": target}
             )
-            for i, (source, target) in enumerate(((k_ref, kbuf), (v_ref, vbuf)))
+            for i, (source, buffer) in enumerate(((k_ref, kbuf), (v_ref, vbuf)))
         ]
 
     def near_copies():
         return [
             remote(
-                source.at[:, cols(0)], target.at[:, cols(1)], kv_tx.at[i, 1], kv_rx.at[i, 1], {"seq": 2}
+                source.at[:, cols(0)], buffer.at[:, cols(1)], i, kv_rx.at[i, 1], {"seq": 2}
             )
-            for i, (source, target) in enumerate(((k_ref, kbuf), (v_ref, vbuf)))
+            for i, (source, buffer) in enumerate(((k_ref, kbuf), (v_ref, vbuf)))
         ]
 
     def far_copies():
         return [
             remote(
-                buffer.at[:, cols(0)], buffer.at[:, cols(0)], kv_tx.at[i, 0], kv_rx.at[i, 0], {"seq": 2}
+                buffer.at[:, cols(0)], buffer.at[:, cols(0)], 2 + i, kv_rx.at[i, 0], {"seq": 2}
             )
             for i, buffer in enumerate((kbuf, vbuf))
         ]
 
-    def query_copy(h, slot, target):
+    def query_copy(h, slot, target, sent):
         return remote(
-            q_ref.at[:, cols(h)], qbuf.at[slot, :, cols(h)],
-            q_tx.at[slot, h], q_rx.at[slot, h], {"seq": target},
+            q_ref.at[:, cols(h)], qbuf.at[slot, :, cols(h)], sent, q_rx.at[slot, h], {"seq": target}
         )
 
     def relay_copy(h):
         return remote(
-            qbuf.at[1, :, cols(h)], qbuf.at[1, :, cols(h)], q_tx.at[1, h], q_rx.at[1, h], {"seq": 1}
+            qbuf.at[1, :, cols(h)], qbuf.at[1, :, cols(h)], 1, q_rx.at[1, h], {"seq": 1}
         )
 
     def level_copy(h, slot):
-        return remote(
-            l_send.at[slot, h], l_recv.at[h], l_tx.at[slot, h], l_rx.at[h], {"seq": 2 + slot}
-        )
+        return remote(l_send.at[slot, h], l_recv.at[h], 5, l_rx.at[h - 1], {"seq": 2 + slot})
 
     def chunk_copy(h, slot, index):
         place = lanes(peer_of(index), share)
         return remote(
-            o_send.at[slot, h, :, place], o_recv.at[h, :, place],
-            o_tx.at[slot, h, index], o_rx.at[h, index], {"seq": 2 + slot},
+            o_send.at[slot, h, :, place], o_recv.at[h, :, place], 6, o_rx.at[h - 1, index],
+            {"seq": 2 + slot},
         )
 
     def part_copies(h):
         return (
-            remote(l_send.at[1, h], l_part.at[h], p_tx.at[0, h], p_rx.at[0, h], {"seq": 3}),
-            remote(o_send.at[1, h], o_part.at[h], p_tx.at[1, h], p_rx.at[1, h], {"seq": 3}),
-        )
-
-    def state_copy(h, tx_slot, in_slot, target):
+            remote(l_send.at[1, h], l_part.at[h], 5, q_rx.at[0, h], {"seq": 3}),
+            remote(o_send.at[1, h], o_part.at[h], 6, q_rx.at[1, h], {"seq": 3}),
+        )
+
+    def state_copy(h, slot, target):
         return remote(
-            s_send.at[h], s_recv.at[in_slot, h], s_tx.at[tx_slot, h], s_rx.at[in_slot, h],
-            {"seq": target},
+            s_send.at[h], s_recv.at[slot, h], 4, s_rx.at[slot, h], {"seq": target}
         )
 
     def prefix_copy(h):
         return remote(
-            s_recv.at[0, h], s_recv.at[0, h], s_tx.at[1, h], s_rx.at[0, h], {"seq": 3}
+            s_recv.at[0, h], s_recv.at[0, h], 7, s_rx.at[0, h], {"seq": 3}
         )
 
     def mixed_copy(h, index):
         target = peer_of(index)
         return remote(
             mixed.at[cols(h), lanes(target, share)], gathered.at[h, lanes(here, HD), :],
-            m_tx.at[h, index], m_rx.at[h, index], {"head": target},
-        )
-
-    def loop(body, first=0):
-        lax.fori_loop(first, heads, lambda h, c: (body(h), c)[1], 0)
+            8, m_rx.at[h], {"head": target},
+        )
+
+    def loop(body, first=0, last=heads):
+        lax.fori_loop(first, last, lambda h, c: (body(h), c)[1], 0)
 
     causal = lax.broadcasted_iota(jnp.int32, (length, length), 0) <= lax.broadcasted_iota(
         jnp.int32, (length, length), 1
@@ -240,19 +239,15 @@
 
     tile = math.gcd(w_ref.shape[2], 512)
 
-    def project(h):
-        for peer in range(peers):
-            load_w(h, peer).wait()
-        for index in range(1, peers):
-            mixed_copy(h, index).wait()
+    def project(h, target=None):
+        settle(w_ref.at[h], w_sem.at[h])
+        settle(gathered.at[h, pl.ds(0, (peers - 1) * HD)], m_rx.at[h])
         left = gathered[h].T
-
-        @pl.loop(0, w_ref.shape[2] // tile)
-        def _(index):
-            part_cols = lanes(index, tile)
-            summed[:, part_cols] += jnp.dot(
-                left, w_ref[h, :, part_cols], preferred_element_type=F32
-            )
+        target = summed if target is None else target
+        for begin in range(0, w_ref.shape[2], tile):
+            piece = slice(begin, begin + tile)
+            product = jnp.dot(left, w_ref[h, :, piece], preferred_element_type=F32)
+            target[:, piece] = (summed[:, piece] + product).astype(target.dtype)
 
     def project_before(h):
         @pl.when(h > 0)
@@ -262,6 +257,10 @@
     def weights():
         lax.fori_loop(0, heads, lambda h, c: (load_head(h), c)[1], 0)
         summed[...] = jnp.zeros_like(summed)
+
+    direct = range(1, heads - 1)
+    wide = [0, heads - 1]
+    later = pl.ds(1, heads - 1)
 
     @pl.when(seq == 0)
     def _():
@@ -270,35 +269,24 @@
                 copy.start()
 
         def work(h):
-            own(h)
             finish(h, acc[h], lin[h])
             project_before(h)
-
-        def drain(h):
-            kv_copies(h)[1].wait_send()
-
-            @pl.when(h > 0)
-            def _():
-                kv_copies(h)[0].wait_send()
 
         @pl.when(core == 0)
         def _():
             loop(send)
-            kv_copies(0)[0].wait_send()
-            pl.semaphore_signal(
-                turn, inc=1, device_id={"head": peer_of(1)}, device_id_type=MESH
-            )
-
-        weights()
+
+        loop(own, 0, 2)
 
         @pl.when(core == 1)
         def _():
-            pl.semaphore_wait(turn, 1)
             loop(send)
-            kv_copies(0)[0].wait_send()
-
+
+        weights()
+        loop(own, 2)
         loop(work)
-        loop(drain)
+        settle(k_ref, tx.at[0])
+        settle(v_ref, tx.at[1])
 
     @pl.when(seq == 1)
     def _():
@@ -309,7 +297,7 @@
 
         def pre(h):
             for slot in range(2):
-                query_copy(h, slot, 1).wait_recv()
+                query_copy(h, slot, 1, 0).wait_recv()
                 bottom, output = part(
                     qbuf[slot, :, cols(h)], ((k_ref[:, cols(h)], v_ref[:, cols(h)]),)
                 )
@@ -344,7 +332,7 @@
             arrived[1].wait_recv()
             early = early_state(h)
             s_send[h] = (early + dot_tn(v_ref[:, cols(h)], k_ref[:, cols(h)])).astype(BF16)
-            state_copy(h, 0, 0, 2).start()
+            state_copy(h, 0, 2).start()
             for slot in (1, 0):
                 fresh = dot_tn(vbuf[:, cols(h)], ebuf[slot]) * pstat[slot, 2:3, :]
                 bottom, output = blend(
@@ -353,7 +341,10 @@
                 l_send[slot, h] = bottom
                 o_send[slot, h] = output.astype(BF16)
                 level_copy(h, slot).start()
-                for index in order:
+                for index in order[:-2]:
+                    chunk_copy(h, slot, index).start()
+            for slot in (1, 0):
+                for index in order[-2:]:
                     chunk_copy(h, slot, index).start()
 
             @pl.when(h + 1 < heads)
@@ -363,27 +354,25 @@
             rest(h, early.astype(BF16))
             project(h - 1)
 
-        def drain(h):
-            state_copy(h, 0, 0, 2).wait_send()
-            for slot in range(2):
-                level_copy(h, slot).wait_send()
-                for index in order:
-                    chunk_copy(h, slot, index).wait_send()
-
         loop(work, 1)
         for copy in near_copies() + far_copies():
             copy.wait_send()
-        loop(drain, 1)
+        settle(s_send.at[later], tx.at[4])
+        settle(l_send.at[:, later], tx.at[5])
+        settle(o_send.at[:, later], tx.at[6])
 
     @pl.when(seq == 2)
     def _():
-        loop(lambda h: query_copy(h, 0, 1).start(), 1)
+        for h in range(1, heads):
+            query_copy(h, 0, 1, 0).start()
+        for h in direct:
+            for copy in kv_copies(h, 3, 2):
+                copy.start()
         weights()
-
-        def first(h):
-            own(h)
+        loop(own)
+        for h in wide:
             s_send[h] = dot_tn(v_ref[:, cols(h)], k_ref[:, cols(h)]).astype(BF16)
-            state_copy(h, 0, 1, 3).start()
+            state_copy(h, 1, 3).start()
 
         def emit(h, pairs):
             bottom, output = part(qbuf[1, :, cols(h)], pairs)
@@ -392,79 +381,92 @@
             for copy in part_copies(h):
                 copy.start()
 
-        def middle(h):
-            query_copy(h, 1, 2).wait_recv()
-            relay_copy(h).start()
-            emit(h, ((k_ref[:, cols(h)], v_ref[:, cols(h)]),))
-
-        loop(first)
-        loop(middle, 1)
-        query_copy(0, 1, 2).wait_recv()
+        def pair(h):
+            return k_ref[:, cols(h)], v_ref[:, cols(h)]
+
+        query_copy(heads - 1, 1, 2, 0).wait_recv()
+        relay_copy(heads - 1).start()
+        emit(heads - 1, (pair(heads - 1),))
+        query_copy(0, 1, 2, 0).wait_recv()
         for copy in near_copies() + far_copies():
             copy.wait_recv()
         pairs = [(kbuf[:, cols(i)], vbuf[:, cols(i)]) for i in range(2)]
         s_recv[0, 0] = sum(dot_tn(value, key) for key, value in pairs).astype(BF16)
         prefix_copy(0).start()
-        emit(0, pairs + [(k_ref[:, cols(0)], v_ref[:, cols(0)])])
+        emit(0, pairs + [pair(0)])
         query = q_ref[:, cols(0)]
         windowed = blend(current(0), part(query, pairs))[1]
         finish(0, windowed, lin[0] + dot_nt(s_recv[0, 0], query))
 
         def second(h):
-            state_copy(h, 0, 0, 2).wait_recv()
+            state_copy(h, 0, 2).wait_recv()
             prefix_copy(h).start()
             lin[h] = norm(lin[h] + dot_nt(s_recv[0, h], q_ref[:, cols(h)]))
             arrive(h)
             project(h - 1)
 
-        def drain(h):
-            @pl.when(h > 0)
-            def _():
-                query_copy(h, 0, 1).wait_send()
-                relay_copy(h).wait_send()
-
-            state_copy(h, 0, 1, 3).wait_send()
-            prefix_copy(h).wait_send()
-            for copy in part_copies(h):
-                copy.wait_send()
-
         loop(second, 1)
-        loop(drain)
+        settle(q_ref.at[:, pl.ds(HD, width - HD)], tx.at[0])
+        relay_copy(heads - 1).wait_send()
+        if len(direct):
+            inner = pl.ds(HD, width - 2 * HD)
+            settle(k_ref.at[:, inner], tx.at[2])
+            settle(v_ref.at[:, inner], tx.at[3])
+        settle(s_send.at[pl.ds(0, 2)], tx.at[4])
+        settle(l_send.at[1, pl.ds(0, 2)], tx.at[5])
+        settle(o_send.at[1, pl.ds(0, 2)], tx.at[6])
+        settle(s_recv.at[0], tx.at[7])
 
     @pl.when(seq == 3)
     def _():
-        for h in [1, 0] + list(range(2, heads)):
-            query_copy(h, 1, 2).start()
+        for h in sorted(range(heads), key=lambda h: h if h else 1.5):
+            if h in direct:
+                query_copy(h, 1, 1, 0).start()
+            else:
+                query_copy(h, 1, 2, 1).start()
         weights()
         loop(own)
 
         def join(h):
-            for copy in part_copies(h):
-                copy.wait_recv()
-            bottom, output = blend(current(h), (l_part[h], o_part[h].astype(F32)))
+            query = q_ref[:, cols(h)]
+            if h in direct:
+                for copy in kv_copies(h, 3, 2):
+                    copy.wait_recv()
+                key, value = kbuf[:, cols(h)], vbuf[:, cols(h)]
+                extra = part(query, ((key, value),))
+                step = dot_tn(value, key).astype(BF16)
+            else:
+                for copy in part_copies(h):
+                    copy.wait_recv()
+                state_copy(h, 1, 3).wait_recv()
+                extra = l_part[h], o_part[h].astype(F32)
+                step = s_recv[1, h]
+            bottom, output = blend(current(h), extra)
             stat[h, 0:1, :] = bottom
             acc[h] = output
-            state_copy(h, 0, 1, 3).wait_recv()
-            lin[h] += dot_nt(s_recv[1, h], q_ref[:, cols(h)])
+            lin[h] += dot_nt(step, query)
 
         def linear(h):
             prefix_copy(h).wait_recv()
             return lin[h] + dot_nt(s_recv[0, h], q_ref[:, cols(h)])
-
-        loop(join, 1)
-        join(0)
-        finish(0, acc[0], linear(0))
 
         def work(h):
             lin[h] = norm(linear(h))
             arrive(h)
             project(h - 1)
 
+        for h in direct:
+            join(h)
+        join(heads - 1)
+        join(0)
+        finish(0, acc[0], linear(0))
         loop(work, 1)
-        loop(lambda h: query_copy(h, 1, 2).wait_send())
-
-    project(heads - 1)
-    out_ref[...] = summed[...].astype(BF16)
+        if len(direct):
+            settle(q_ref.at[:, pl.ds(HD, width - 2 * HD)], tx.at[0])
+        settle(q_ref.at[:, pl.ds(0, 2 * HD)], tx.at[1])
+
+    project(heads - 1, out_ref)
+    settle(mixed.at[:, pl.ds(0, length - share)], tx.at[8])
 
 
 def fused(queries, keys, values, w_out):
@@ -476,7 +478,7 @@
     vmem = pl.BlockSpec(memory_space=pltpu.VMEM)
     return pl.pallas_call(
         functools.partial(kernel, peers),
-        out_shape=jax.ShapeDtypeStruct((share, w_out.shape[1]), BF16),
+        out_shape=pltpu.VMEM((share, w_out.shape[1]), BF16),
         in_specs=[pl.BlockSpec(memory_space=pltpu.HBM)] * 4,
         out_specs=vmem,
         scratch_shapes=[
@@ -504,10 +506,8 @@
             pltpu.VMEM((heads, 8, length), F32),
             pltpu.VMEM((width, length), BF16),
             pltpu.VMEM((heads, peers * HD, share), BF16),
-            dma((3,)), dma((heads, peers)), dma((2, heads)), dma((2, heads)), dma((2, heads)), dma((2, heads)),
-            dma((2, heads, peers)), dma((heads, peers)), dma((2, heads)), dma((heads,)), dma((2, heads)), dma((2, heads)),
-            dma((2, heads)), dma((2, heads)), dma((heads, peers)), dma((heads, peers)),
-            pltpu.SemaphoreType.REGULAR,
+            dma((3,)), dma((heads,)), dma((9,)), dma((2, heads)), dma((2, heads)), dma((heads - 1, peers)),
+            dma((heads - 1,)), dma((2, heads)), dma((heads,)),
         ],
         compiler_params=pltpu.CompilerParams(
             collective_id=0, has_side_effects=True, vmem_limit_bytes=56 * 1024 * 1024

time: 46.3 us -> 40.8 us (0.88); the launches traced: 45.5 us -> 40.6 us
  Pallas kernels: 43.6 us -> 39.8 us
  local copies, waits for them, and re-layouts: 1.88 us -> 0.8 us
    pallas_call x1, Pallas kernels: 43.6 us -> 39.8 us  [fused(): pl.pallas_call(functools.partial(kernel, peers), out_shape=pltpu.VMEM((sh...]
    unnamed x1, local copies, waits for them, and re-layouts: 1.88 us -> 0.8 us
where the time goes in v2:
time: 40.8 us; the launch traced here: 40.6 us
  Pallas kernels  39.8 us (98%)
  local copies, waits for them, and re-layouts  0.8 us (2%)
    pallas_call x1, Pallas kernels, fused(): pl.pallas_call(functools.partial(kernel, peers), out_shape=pltpu.VMEM((sh...  39.8 us

profile of v2, /device:TPU:25, one launch (start us, length us, event | category | flops | bytes accessed | tf_op | source)
XLA Modules:
  0.0 40.6 jit_solution(7858652852007509250)
XLA Ops:
  0.0 39.8 %shard_map.46 = bf16[128,2048]{1,0:T(8,128)(2,1)S(1)} custom-call(bf16[512,512]{1,0:T(8,128)(2,1)} %q_hbm.1, bf16[512,512]{1,0:T(8,128)(2,1)} %k_hbm.1, bf16[512,512]{1,0:T(8,128)(2,1)} %v_hbm.1, bf16[2048,2048]{1,0:T(8,128)(2,1)} %w_hbm.1), custom_call_target="tpu_custom_call" | custom-call | tf_op jit(solution)/shard_map/pallas_call | solution.py:479
  39.8 0.8 %copy.6 = bf16[128,2048]{1,0:T(8,128)(2,1)} copy(bf16[128,2048]{1,0:T(8,128)(2,1)S(1)} %shard_map.46) | data formatting | bytes 1048576

commit v3 on v2

--- a/solution.py
+++ b/solution.py
@@ -35,9 +35,9 @@
 
 def kernel(
     peers, q_hbm, k_hbm, v_hbm, w_hbm, out_ref, q_ref, k_ref, v_ref,
-    w_ref, summed, kbuf, vbuf, qbuf, ebuf, pacc, pstat, o_send, o_recv, o_part, l_send, l_recv, l_part,
-    s_send, s_recv, acc, lin, stat, mixed, gathered,
-    in_sem, w_sem, tx, kv_rx, q_rx, o_rx, l_rx, s_rx, m_rx,
+    w_ref, summed, kbuf, vbuf, qbuf, ebuf, pacc, pstat, o_send, o_recv, l_send, l_recv,
+    s_own, s_send, s_recv, acc, lin, stat, mixed, gathered,
+    in_sem, w_sem, tx, kv_rx, q_rx, o_rx, l_rx, s_rx, m_rx, gate,
 ):
     seq = lax.axis_index("seq")
     here = lax.axis_index("head")
@@ -58,14 +58,16 @@
     def greet(device):
         pl.semaphore_signal(barrier, inc=1, device_id=device, device_id_type=MESH)
 
-    for index in range(1, peers):
-        greet({"head": peer_of(index)})
-    circle = {0: (1,), 1: (0, 2, 3), 2: (1, 3), 3: (1, 2)}
+    circle = {0: (1,), 1: (0, 2, 3), 2: (1, 3), 3: (2,)}
+    near = {0: (1,), 1: (), 2: range(1, peers), 3: range(1, peers)}
     for place, friends in circle.items():
         @pl.when(seq == place)
         def _():
             for friend in friends:
                 greet({"seq": friend})
+
+            for index in near[place]:
+                greet({"head": peer_of(index)})
 
     loads = [
         pltpu.make_async_copy(source, target, in_sem.at[i])
@@ -85,10 +87,11 @@
         for peer in range(peers):
             load_w(h, peer).start()
 
-    for place, friends in circle.items():
+    for place in circle:
         @pl.when(seq == place)
         def _():
-            pl.semaphore_wait(barrier, len(friends) + peers - 1)
+            count = sum(place in friends for friends in circle.values())
+            pl.semaphore_wait(barrier, count + len(near[place]))
     for load in loads:
         load.wait()
 
@@ -104,10 +107,10 @@
     def settle(ref, semaphore):
         pltpu.make_async_copy(ref, ref, semaphore).wait()
 
-    def kv_copies(h, target=1, first=0):
+    def kv_copies(h):
         return [
             remote(
-                source.at[:, cols(h)], buffer.at[:, cols(h)], first + i, kv_rx.at[i, h], {"seq": target}
+                source.at[:, cols(h)], buffer.at[:, cols(h)], i, kv_rx.at[i, h], {"seq": 1}
             )
             for i, (source, buffer) in enumerate(((k_ref, kbuf), (v_ref, vbuf)))
         ]
@@ -138,31 +141,39 @@
             qbuf.at[1, :, cols(h)], qbuf.at[1, :, cols(h)], 1, q_rx.at[1, h], {"seq": 1}
         )
 
+    def row(h, slot):
+        return slot * (heads - 1) + h - 1
+
     def level_copy(h, slot):
-        return remote(l_send.at[slot, h], l_recv.at[h], 5, l_rx.at[h - 1], {"seq": 2 + slot})
+        return remote(
+            l_send.at[slot, h], l_recv.at[slot, h], 5, l_rx.at[row(h, slot)], {"seq": 2}
+        )
 
     def chunk_copy(h, slot, index):
         place = lanes(peer_of(index), share)
         return remote(
-            o_send.at[slot, h, :, place], o_recv.at[h, :, place], 6, o_rx.at[h - 1, index],
-            {"seq": 2 + slot},
-        )
-
-    def part_copies(h):
+            o_send.at[slot, h, :, place], o_recv.at[slot, h, :, place], 6,
+            o_rx.at[row(h, slot), index], {"seq": 2},
+        )
+
+    def level_onward(h):
+        return remote(l_send.at[1, h], l_recv.at[1, h], 5, l_rx.at[h], {"seq": 3})
+
+    def chunk_onward(h, index):
+        place = lanes(peer_of(index), share)
+        return remote(
+            o_send.at[1, h, :, place], o_recv.at[1, h, :, place], 6, o_rx.at[h, index], {"seq": 3}
+        )
+
+    def part_copies():
+        h = heads - 1
         return (
-            remote(l_send.at[1, h], l_part.at[h], 5, q_rx.at[0, h], {"seq": 3}),
-            remote(o_send.at[1, h], o_part.at[h], 6, q_rx.at[1, h], {"seq": 3}),
-        )
-
-    def state_copy(h, slot, target):
-        return remote(
-            s_send.at[h], s_recv.at[slot, h], 4, s_rx.at[slot, h], {"seq": target}
-        )
-
-    def prefix_copy(h):
-        return remote(
-            s_recv.at[0, h], s_recv.at[0, h], 7, s_rx.at[0, h], {"seq": 3}
-        )
+            remote(l_send.at[0, h], l_recv.at[0, h], 2, q_rx.at[0, 0], {"seq": 3}),
+            remote(o_send.at[0, h], o_recv.at[0, h], 3, q_rx.at[1, 0], {"seq": 3}),
+        )
+
+    def state_copy(h, target):
+        return remote(s_send.at[h], s_recv.at[h], 4, s_rx.at[h], {"seq": target})
 
     def mixed_copy(h, index):
         target = peer_of(index)
@@ -223,13 +234,15 @@
             mixed_copy(h, index).start()
         gathered[h, lanes(here, HD), :] = mixed[cols(h), lanes(here, share)]
 
-    def arrive(h):
-        level_copy(h, 0).wait_recv()
+    def arrive(h, slot, level_of, chunk_of, final=False):
+        level_of(h).wait_recv()
         for index in order:
-            chunk_copy(h, 0, index).wait_recv()
+            if final and index == order[-2]:
+                project_before(h)
+            chunk_of(h, index).wait_recv()
             place = lanes(peer_of(index), share)
             mine = stat[h, 0:1, place], acc[h, :, place]
-            theirs = l_recv[h, 0:1, place], o_recv[h, :, place].astype(F32)
+            theirs = l_recv[slot, h, 0:1, place], o_recv[slot, h, :, place].astype(F32)
             piece = (lin[h, :, place] + blend(mine, theirs)[1]).astype(BF16)
             if index:
                 mixed[cols(h), place] = piece
@@ -250,16 +263,21 @@
             target[:, piece] = (summed[:, piece] + product).astype(target.dtype)
 
     def project_before(h):
-        @pl.when(h > 0)
-        def _():
+        if isinstance(h, int):
             project(h - 1)
+        else:
+            pl.when(h > 0)(lambda: project(h - 1))
 
     def weights():
         lax.fori_loop(0, heads, lambda h, c: (load_head(h), c)[1], 0)
         summed[...] = jnp.zeros_like(summed)
 
-    direct = range(1, heads - 1)
-    wide = [0, heads - 1]
+    def tell(slot, device):
+        pl.semaphore_signal(gate.at[slot], inc=1, device_id=device, device_id_type=MESH)
+
+    def own_state(h):
+        return dot_tn(v_ref[:, cols(h)], k_ref[:, cols(h)])
+
     later = pl.ds(1, heads - 1)
 
     @pl.when(seq == 0)
@@ -275,6 +293,13 @@
         @pl.when(core == 0)
         def _():
             loop(send)
+            tell(1, {"head": peer_of(1)})
+
+        weights()
+
+        @pl.when(core == 1)
+        def _():
+            pl.semaphore_wait(gate.at[1], 1)
 
         loop(own, 0, 2)
 
@@ -282,8 +307,8 @@
         def _():
             loop(send)
 
-        weights()
         loop(own, 2)
+        pl.semaphore_wait(gate.at[0], 1)
         loop(work)
         settle(k_ref, tx.at[0])
         settle(v_ref, tx.at[1])
@@ -292,8 +317,14 @@
     def _():
         for copy in near_copies():
             copy.start()
+        tell(0, {"seq": 2})
         weights()
-        loop(own)
+
+        def first(h):
+            own(h)
+            s_own[h] = own_state(h)
+
+        loop(first)
 
         def pre(h):
             for slot in range(2):
@@ -315,10 +346,12 @@
         for arrived, onward in zip(kv_copies(0), far_copies()):
             arrived.wait_recv()
             onward.start()
+        pl.semaphore_wait(gate.at[0], 1)
+        tell(0, {"seq": 0})
         rest(0, early_state(0).astype(BF16))
         pre(1)
 
-        def work(h):
+        def work(h, final=False):
             arrived = kv_copies(h)
             arrived[0].wait_recv()
             for slot in range(2):
@@ -331,8 +364,8 @@
                 ebuf[slot] = expo.astype(BF16)
             arrived[1].wait_recv()
             early = early_state(h)
-            s_send[h] = (early + dot_tn(v_ref[:, cols(h)], k_ref[:, cols(h)])).astype(BF16)
-            state_copy(h, 0, 2).start()
+            s_send[h] = (early + s_own[h]).astype(BF16)
+            state_copy(h, 2).start()
             for slot in (1, 0):
                 fresh = dot_tn(vbuf[:, cols(h)], ebuf[slot]) * pstat[slot, 2:3, :]
                 bottom, output = blend(
@@ -340,21 +373,21 @@
                 )
                 l_send[slot, h] = bottom
                 o_send[slot, h] = output.astype(BF16)
-                level_copy(h, slot).start()
-                for index in order[:-2]:
-                    chunk_copy(h, slot, index).start()
-            for slot in (1, 0):
+                straight = final and slot
+                (level_onward(h) if straight else level_copy(h, slot)).start()
+                for index in order[:-2] if final else order:
+                    (chunk_onward(h, index) if straight else chunk_copy(h, slot, index)).start()
+            if final:
                 for index in order[-2:]:
-                    chunk_copy(h, slot, index).start()
-
-            @pl.when(h + 1 < heads)
-            def _():
+                    chunk_onward(h, index).start()
+                    chunk_copy(h, 0, index).start()
+            else:
                 pre(h + 1)
-
             rest(h, early.astype(BF16))
             project(h - 1)
 
-        loop(work, 1)
+        loop(work, 1, heads - 1)
+        work(heads - 1, True)
         for copy in near_copies() + far_copies():
             copy.wait_send()
         settle(s_send.at[later], tx.at[4])
@@ -363,107 +396,134 @@
 
     @pl.when(seq == 2)
     def _():
-        for h in range(1, heads):
+        for h in range(1, min(3, heads)):
             query_copy(h, 0, 1, 0).start()
-        for h in direct:
-            for copy in kv_copies(h, 3, 2):
-                copy.start()
         weights()
-        loop(own)
-        for h in wide:
-            s_send[h] = dot_tn(v_ref[:, cols(h)], k_ref[:, cols(h)]).astype(BF16)
-            state_copy(h, 1, 3).start()
-
-        def emit(h, pairs):
-            bottom, output = part(qbuf[1, :, cols(h)], pairs)
-            l_send[1, h] = bottom
-            o_send[1, h] = output.astype(BF16)
-            for copy in part_copies(h):
-                copy.start()
+
+        def first(h):
+            own(h)
+            s_own[h] = own_state(h)
+
+        loop(first, 0, 2)
+        pl.semaphore_wait(gate.at[0], 1)
+        for index in range(1, peers):
+            tell(1, {"head": peer_of(index)})
+        loop(first, 2)
+        pl.semaphore_wait(gate.at[1], peers - 1)
+        tell(0, {"seq": 1})
 
         def pair(h):
             return k_ref[:, cols(h)], v_ref[:, cols(h)]
 
-        query_copy(heads - 1, 1, 2, 0).wait_recv()
-        relay_copy(heads - 1).start()
-        emit(heads - 1, (pair(heads - 1),))
-        query_copy(0, 1, 2, 0).wait_recv()
+        def third(h):
+            query_copy(h, 1, 2, 0).wait_recv()
+            if h > 1:
+                relay_copy(h).start()
+                if h + 1 < heads:
+                    query_copy(h + 1, 0, 1, 0).start()
+            if h:
+                bottom, output = part(qbuf[1, :, cols(h)], (pair(h),))
+                if h < heads - 1:
+                    pstat[h, 0:1, :] = bottom
+                    pacc[h] = output
+                else:
+                    l_send[0, h] = bottom
+                    o_send[0, h] = output.astype(BF16)
+                    for copy in part_copies():
+                        copy.start()
+
+        for h in [*range(2, heads), 0]:
+            third(h)
         for copy in near_copies() + far_copies():
             copy.wait_recv()
         pairs = [(kbuf[:, cols(i)], vbuf[:, cols(i)]) for i in range(2)]
-        s_recv[0, 0] = sum(dot_tn(value, key) for key, value in pairs).astype(BF16)
-        prefix_copy(0).start()
-        emit(0, pairs + [pair(0)])
+        early = sum(dot_tn(value, key) for key, value in pairs)
+        s_send[0] = (early + s_own[0]).astype(BF16)
+        state_copy(0, 3).start()
+        bottom, output = part(qbuf[1, :, cols(0)], pairs + [pair(0)])
+        l_send[1, 0] = bottom
+        o_send[1, 0] = output.astype(BF16)
+        level_onward(0).start()
+        for index in order:
+            chunk_onward(0, index).start()
         query = q_ref[:, cols(0)]
         windowed = blend(current(0), part(query, pairs))[1]
-        finish(0, windowed, lin[0] + dot_nt(s_recv[0, 0], query))
+        finish(0, windowed, lin[0] + dot_nt(early.astype(BF16), query))
+        if heads > 2:
+            third(1)
+
+        def state(h):
+            state_copy(h, 2).wait_recv()
+            s_send[h] = (s_recv[h].astype(F32) + s_own[h]).astype(BF16)
+            state_copy(h, 3).start()
+
+        def close(h):
+            lin[h] = norm(lin[h] + dot_nt(s_recv[h], q_ref[:, cols(h)]))
+            final = isinstance(h, int)
+            arrive(
+                h, 0, lambda h: level_copy(h, 0), lambda h, index: chunk_copy(h, 0, index), final
+            )
+            if not final:
+                project(h - 1)
 
         def second(h):
-            state_copy(h, 0, 2).wait_recv()
-            prefix_copy(h).start()
-            lin[h] = norm(lin[h] + dot_nt(s_recv[0, h], q_ref[:, cols(h)]))
-            arrive(h)
-            project(h - 1)
-
-        loop(second, 1)
+            state(h)
+            level_copy(h, 1).wait_recv()
+            mine, theirs = pstat[h, 0:1, :], l_recv[1, h]
+            top = jnp.maximum(mine, theirs)
+            left, right = jnp.exp2(mine - top), jnp.exp2(theirs - top)
+            total = left + right
+            l_send[1, h] = top + jnp.log2(total)
+            pstat[h, 1:2, :] = left * recip(total)
+            pstat[h, 2:3, :] = right * recip(total)
+            level_onward(h).start()
+            for index in order:
+                chunk_copy(h, 1, index).wait_recv()
+                place = lanes(peer_of(index), share)
+                output = pstat[h, 1:2, place] * pacc[h, :, place]
+                output += pstat[h, 2:3, place] * o_recv[1, h, :, place].astype(F32)
+                o_send[1, h, :, place] = output.astype(BF16)
+                chunk_onward(h, index).start()
+            close(h)
+
+        loop(second, 1, heads - 1)
+        state(heads - 1)
+        close(heads - 1)
+        for copy in part_copies():
+            copy.wait_send()
         settle(q_ref.at[:, pl.ds(HD, width - HD)], tx.at[0])
-        relay_copy(heads - 1).wait_send()
-        if len(direct):
-            inner = pl.ds(HD, width - 2 * HD)
-            settle(k_ref.at[:, inner], tx.at[2])
-            settle(v_ref.at[:, inner], tx.at[3])
-        settle(s_send.at[pl.ds(0, 2)], tx.at[4])
-        settle(l_send.at[1, pl.ds(0, 2)], tx.at[5])
-        settle(o_send.at[1, pl.ds(0, 2)], tx.at[6])
-        settle(s_recv.at[0], tx.at[7])
+        if heads > 2:
+            settle(q_ref.at[:, pl.ds(2 * HD, width - 2 * HD)], tx.at[1])
+        settle(s_send, tx.at[4])
+        settle(l_send.at[1, pl.ds(0, heads - 1)], tx.at[5])
+        settle(o_send.at[1, pl.ds(0, heads - 1)], tx.at[6])
 
     @pl.when(seq == 3)
     def _():
-        for h in sorted(range(heads), key=lambda h: h if h else 1.5):
-            if h in direct:
-                query_copy(h, 1, 1, 0).start()
-            else:
-                query_copy(h, 1, 2, 1).start()
+        query_copy(1, 1, 1, 0).start()
+        for h in [*range(2, heads), 0, 1]:
+            query_copy(h, 1, 2, 1).start()
         weights()
         loop(own)
 
-        def join(h):
-            query = q_ref[:, cols(h)]
-            if h in direct:
-                for copy in kv_copies(h, 3, 2):
-                    copy.wait_recv()
-                key, value = kbuf[:, cols(h)], vbuf[:, cols(h)]
-                extra = part(query, ((key, value),))
-                step = dot_tn(value, key).astype(BF16)
-            else:
-                for copy in part_copies(h):
-                    copy.wait_recv()
-                state_copy(h, 1, 3).wait_recv()
-                extra = l_part[h], o_part[h].astype(F32)
-                step = s_recv[1, h]
-            bottom, output = blend(current(h), extra)
-            stat[h, 0:1, :] = bottom
-            acc[h] = output
-            lin[h] += dot_nt(step, query)
-
-        def linear(h):
-            prefix_copy(h).wait_recv()
-            return lin[h] + dot_nt(s_recv[0, h], q_ref[:, cols(h)])
-
         def work(h):
-            lin[h] = norm(linear(h))
-            arrive(h)
-            project(h - 1)
-
-        for h in direct:
-            join(h)
-        join(heads - 1)
-        join(0)
-        finish(0, acc[0], linear(0))
-        loop(work, 1)
-        if len(direct):
-            settle(q_ref.at[:, pl.ds(HD, width - 2 * HD)], tx.at[0])
-        settle(q_ref.at[:, pl.ds(0, 2 * HD)], tx.at[1])
+            state_copy(h, 3).wait_recv()
+            lin[h] = norm(lin[h] + dot_nt(s_recv[h], q_ref[:, cols(h)]))
+            final = isinstance(h, int)
+            arrive(h, 1, level_onward, chunk_onward, final)
+            if not final:
+                project_before(h)
+
+        loop(work, 0, heads - 1)
+        for copy in part_copies():
+            copy.wait_recv()
+        last = heads - 1
+        bottom, output = blend(current(last), (l_recv[0, last], o_recv[0, last].astype(F32)))
+        stat[last, 0:1, :] = bottom
+        acc[last] = output
+        work(last)
+        query_copy(1, 1, 1, 0).wait_send()
+        settle(q_ref, tx.at[1])
 
     project(heads - 1, out_ref)
     settle(mixed.at[:, pl.ds(0, length - share)], tx.at[8])
@@ -491,23 +551,23 @@
             pltpu.VMEM((length, width), BF16),
             pltpu.VMEM((2, length, width), BF16),
             pltpu.VMEM((2, length, length), BF16),
-            pltpu.VMEM((2, HD, length), F32),
-            pltpu.VMEM((2, 8, length), F32),
+            pltpu.VMEM((heads, HD, length), F32),
+            pltpu.VMEM((heads, 8, length), F32),
             pltpu.VMEM((2, heads, HD, length), BF16),
-            pltpu.VMEM((heads, HD, length), BF16),
-            pltpu.VMEM((heads, HD, length), BF16),
+            pltpu.VMEM((2, heads, HD, length), BF16),
             pltpu.VMEM((2, heads, 1, length), F32),
-            pltpu.VMEM((heads, 1, length), F32),
-            pltpu.VMEM((heads, 1, length), F32),
+            pltpu.VMEM((2, heads, 1, length), F32),
+            pltpu.VMEM((heads, HD, HD), F32),
             pltpu.VMEM((heads, HD, HD), BF16),
-            pltpu.VMEM((2, heads, HD, HD), BF16),
+            pltpu.VMEM((heads, HD, HD), BF16),
             pltpu.VMEM((heads, HD, length), F32),
             pltpu.VMEM((heads, HD, length), F32),
             pltpu.VMEM((heads, 8, length), F32),
             pltpu.VMEM((width, length), BF16),
             pltpu.VMEM((heads, peers * HD, share), BF16),
-            dma((3,)), dma((heads,)), dma((9,)), dma((2, heads)), dma((2, heads)), dma((heads - 1, peers)),
-            dma((heads - 1,)), dma((2, heads)), dma((heads,)),
+            dma((3,)), dma((heads,)), dma((9,)), dma((2, heads)), dma((2, heads)),
+            dma((2 * (heads - 1), peers)), dma((2 * (heads - 1),)), dma((heads,)), dma((heads,)),
+            pltpu.SemaphoreType.REGULAR((2,)),
         ],
         compiler_params=pltpu.CompilerParams(
             collective_id=0, has_side_effects=True, vmem_limit_bytes=56 * 1024 * 1024

time: 40.8 us -> 38.3 us (0.939)
  the two profiles are of different devices: /device:TPU:25 before, /device:TPU:16 now
where the time goes in v3:
time: 38.3 us; the launch traced here: 38.2 us
  Pallas kernels  37.4 us (98%)
  local copies, waits for them, and re-layouts  0.8 us (2%)
    pallas_call x1, Pallas kernels, fused(): pl.pallas_call(functools.partial(kernel, peers), out_shape=pltpu.VMEM((sh...  37.4 us
    unnamed x1, local copies, waits for them, and re-layouts  0.8 us

profile of v3, /device:TPU:16, one launch (start us, length us, event | category | flops | bytes accessed | tf_op | source)
XLA Modules:
  0.0 38.2 jit_solution(10966035326414351121)
XLA Ops:
  0.0 37.4 %shard_map.46 = bf16[128,2048]{1,0:T(8,128)(2,1)S(1)} custom-call(bf16[512,512]{1,0:T(8,128)(2,1)} %q_hbm.1, bf16[512,512]{1,0:T(8,128)(2,1)} %k_hbm.1, bf16[512,512]{1,0:T(8,128)(2,1)} %v_hbm.1, bf16[2048,2048]{1,0:T(8,128)(2,1)} %w_hbm.1), custom_call_target="tpu_custom_call" | custom-call | tf_op jit(solution)/shard_map/pallas_call | solution.py:539
  37.4 0.8 %copy.6 = bf16[128,2048]{1,0:T(8,128)(2,1)} copy(bf16[128,2048]{1,0:T(8,128)(2,1)S(1)} %shard_map.46) | data formatting | bytes 1048576

commit v4 on v3

--- a/solution.py
+++ b/solution.py
@@ -234,11 +234,9 @@
             mixed_copy(h, index).start()
         gathered[h, lanes(here, HD), :] = mixed[cols(h), lanes(here, share)]
 
-    def arrive(h, slot, level_of, chunk_of, final=False):
+    def arrive(h, slot, level_of, chunk_of):
         level_of(h).wait_recv()
         for index in order:
-            if final and index == order[-2]:
-                project_before(h)
             chunk_of(h, index).wait_recv()
             place = lanes(peer_of(index), share)
             mine = stat[h, 0:1, place], acc[h, :, place]
@@ -263,10 +261,7 @@
             target[:, piece] = (summed[:, piece] + product).astype(target.dtype)
 
     def project_before(h):
-        if isinstance(h, int):
-            project(h - 1)
-        else:
-            pl.when(h > 0)(lambda: project(h - 1))
+        pl.when(h > 0)(lambda: project(h - 1))
 
     def weights():
         lax.fori_loop(0, heads, lambda h, c: (load_head(h), c)[1], 0)
@@ -278,7 +273,8 @@
     def own_state(h):
         return dot_tn(v_ref[:, cols(h)], k_ref[:, cols(h)])
 
-    later = pl.ds(1, heads - 1)
+    last = heads - 1
+    later = pl.ds(1, last)
 
     @pl.when(seq == 0)
     def _():
@@ -290,28 +286,31 @@
             finish(h, acc[h], lin[h])
             project_before(h)
 
+        @pl.when(core == 1)
+        def _():
+            loop(send, 0, 2)
+            tell(1, {"head": peer_of(1)})
+
         @pl.when(core == 0)
         def _():
-            loop(send)
-            tell(1, {"head": peer_of(1)})
-
+            pl.semaphore_wait(gate.at[1], 1)
+
+        own(0)
+
+        @pl.when(core == 0)
+        def _():
+            loop(send, 0, 2)
+
+        s_send[last] = own_state(last).astype(BF16)
+        state_copy(last, 1).start()
+        loop(send, 2)
         weights()
-
-        @pl.when(core == 1)
-        def _():
-            pl.semaphore_wait(gate.at[1], 1)
-
-        loop(own, 0, 2)
-
-        @pl.when(core == 1)
-        def _():
-            loop(send)
-
-        loop(own, 2)
+        loop(own, 1)
         pl.semaphore_wait(gate.at[0], 1)
         loop(work)
         settle(k_ref, tx.at[0])
         settle(v_ref, tx.at[1])
+        state_copy(last, 1).wait_send()
 
     @pl.when(seq == 1)
     def _():
@@ -350,6 +349,11 @@
         tell(0, {"seq": 0})
         rest(0, early_state(0).astype(BF16))
         pre(1)
+
+        def early_last():
+            state_copy(last, 1).wait_recv()
+            s_send[last] = (s_recv[last].astype(F32) + s_own[last]).astype(BF16)
+            state_copy(last, 2).start()
 
         def work(h, final=False):
             arrived = kv_copies(h)
@@ -363,9 +367,13 @@
                 pstat[slot, 2:3, :] = recip(total)
                 ebuf[slot] = expo.astype(BF16)
             arrived[1].wait_recv()
-            early = early_state(h)
-            s_send[h] = (early + s_own[h]).astype(BF16)
-            state_copy(h, 2).start()
+            if final:
+                early = s_recv[h]
+            else:
+                early = early_state(h)
+                s_send[h] = (early + s_own[h]).astype(BF16)
+                state_copy(h, 2).start()
+                early = early.astype(BF16)
             for slot in (1, 0):
                 fresh = dot_tn(vbuf[:, cols(h)], ebuf[slot]) * pstat[slot, 2:3, :]
                 bottom, output = blend(
@@ -382,12 +390,19 @@
                     chunk_onward(h, index).start()
                     chunk_copy(h, 0, index).start()
             else:
+                @pl.when(h == 1)
+                def _():
+                    early_last()
+
                 pre(h + 1)
-            rest(h, early.astype(BF16))
+
+            rest(h, early)
             project(h - 1)
 
-        loop(work, 1, heads - 1)
-        work(heads - 1, True)
+        if last == 1:
+            early_last()
+        loop(work, 1, last)
+        work(last, True)
         for copy in near_copies() + far_copies():
             copy.wait_send()
         settle(s_send.at[later], tx.at[4])
@@ -457,14 +472,11 @@
             s_send[h] = (s_recv[h].astype(F32) + s_own[h]).astype(BF16)
             state_copy(h, 3).start()
 
+            lin[h] = norm(lin[h] + dot_nt(s_recv[h], q_ref[:, cols(h)]))
+
         def close(h):
-            lin[h] = norm(lin[h] + dot_nt(s_recv[h], q_ref[:, cols(h)]))
-            final = isinstance(h, int)
-            arrive(
-                h, 0, lambda h: level_copy(h, 0), lambda h, index: chunk_copy(h, 0, index), final
-            )
-            if not final:
-                project(h - 1)
+            arrive(h, 0, lambda h: level_copy(h, 0), lambda h, index: chunk_copy(h, 0, index))
+            project(h - 1)
 
         def second(h):
             state(h)
@@ -484,11 +496,15 @@
                 output += pstat[h, 2:3, place] * o_recv[1, h, :, place].astype(F32)
                 o_send[1, h, :, place] = output.astype(BF16)
                 chunk_onward(h, index).start()
+
+            @pl.when(h == 1)
+            def _():
+                state(last)
+
             close(h)
 
-        loop(second, 1, heads - 1)
-        state(heads - 1)
-        close(heads - 1)
+        loop(second, 1, last)
+        close(last)
         for copy in part_copies():
             copy.wait_send()
         settle(q_ref.at[:, pl.ds(HD, width - HD)], tx.at[0])
@@ -506,22 +522,24 @@
         weights()
         loop(own)
 
-        def work(h):
+        def state(h):
             state_copy(h, 3).wait_recv()
             lin[h] = norm(lin[h] + dot_nt(s_recv[h], q_ref[:, cols(h)]))
-            final = isinstance(h, int)
-            arrive(h, 1, level_onward, chunk_onward, final)
-            if not final:
-                project_before(h)
-
-        loop(work, 0, heads - 1)
+
+        def work(h):
+            state(h)
+            arrive(h, 1, level_onward, chunk_onward)
+            project_before(h)
+
+        loop(work, 0, last)
+        state(last)
         for copy in part_copies():
             copy.wait_recv()
-        last = heads - 1
         bottom, output = blend(current(last), (l_recv[0, last], o_recv[0, last].astype(F32)))
         stat[last, 0:1, :] = bottom
         acc[last] = output
-        work(last)
+        arrive(last, 1, level_onward, chunk_onward)
+        project(last - 1)
         query_copy(1, 1, 1, 0).wait_send()
         settle(q_ref, tx.at[1])
 

time: 38.3 us -> 37.5 us (0.979)
  the two profiles are of different devices: /device:TPU:16 before, /device:TPU:17 now
where the time goes in v4:
time: 37.5 us; the launch traced here: 37.3 us
  Pallas kernels  36.5 us (97%)
  local copies, waits for them, and re-layouts  0.8 us (2%)
    pallas_call x1, Pallas kernels, fused(): pl.pallas_call(functools.partial(kernel, peers), out_shape=pltpu.VMEM((sh...  36.5 us
    unnamed x1, local copies, waits for them, and re-layouts  0.8 us

profile of v4, /device:TPU:17, one launch (start us, length us, event | category | flops | bytes accessed | tf_op | source)
XLA Modules:
  0.0 37.3 jit_solution(17540549655135934368)
XLA Ops:
  0.0 36.5 %shard_map.46 = bf16[128,2048]{1,0:T(8,128)(2,1)S(1)} custom-call(bf16[512,512]{1,0:T(8,128)(2,1)} %q_hbm.1, bf16[512,512]{1,0:T(8,128)(2,1)} %k_hbm.1, bf16[512,512]{1,0:T(8,128)(2,1)} %v_hbm.1, bf16[2048,2048]{1,0:T(8,128)(2,1)} %w_hbm.1), custom_call_target="tpu_custom_call" | custom-call | tf_op jit(solution)/shard_map/pallas_call | solution.py:557
  36.5 0.8 %copy.6 = bf16[128,2048]{1,0:T(8,128)(2,1)} copy(bf16[128,2048]{1,0:T(8,128)(2,1)S(1)} %shard_map.46) | data formatting | bytes 1048576

commit v5 on v4

--- a/solution.py
+++ b/solution.py
@@ -47,6 +47,8 @@
     chip, core = here // 2, here % 2
     chips = peers // 2
     order = list(range(2, peers)) + [1, 0]
+    last = heads - 1
+    inner = last - 1
 
     def peer_of(index, sign=1):
         hop, flip = index // 2, index % 2
@@ -107,10 +109,11 @@
     def settle(ref, semaphore):
         pltpu.make_async_copy(ref, ref, semaphore).wait()
 
-    def kv_copies(h):
+    def kv_copies(h, first=0, target=1):
         return [
             remote(
-                source.at[:, cols(h)], buffer.at[:, cols(h)], i, kv_rx.at[i, h], {"seq": 1}
+                source.at[:, cols(h)], buffer.at[:, cols(h)], first + i, kv_rx.at[i, h],
+                {"seq": target},
             )
             for i, (source, buffer) in enumerate(((k_ref, kbuf), (v_ref, vbuf)))
         ]
@@ -136,11 +139,6 @@
             q_ref.at[:, cols(h)], qbuf.at[slot, :, cols(h)], sent, q_rx.at[slot, h], {"seq": target}
         )
 
-    def relay_copy(h):
-        return remote(
-            qbuf.at[1, :, cols(h)], qbuf.at[1, :, cols(h)], 1, q_rx.at[1, h], {"seq": 1}
-        )
-
     def row(h, slot):
         return slot * (heads - 1) + h - 1
 
@@ -165,13 +163,6 @@
             o_send.at[1, h, :, place], o_recv.at[1, h, :, place], 6, o_rx.at[h, index], {"seq": 3}
         )
 
-    def part_copies():
-        h = heads - 1
-        return (
-            remote(l_send.at[0, h], l_recv.at[0, h], 2, q_rx.at[0, 0], {"seq": 3}),
-            remote(o_send.at[0, h], o_recv.at[0, h], 3, q_rx.at[1, 0], {"seq": 3}),
-        )
-
     def state_copy(h, target):
         return remote(s_send.at[h], s_recv.at[h], 4, s_rx.at[h], {"seq": target})
 
@@ -179,7 +170,7 @@
         target = peer_of(index)
         return remote(
             mixed.at[cols(h), lanes(target, share)], gathered.at[h, lanes(here, HD), :],
-            8, m_rx.at[h], {"head": target},
+            8, m_rx.at[h + h // last if index == 1 else h], {"head": target},
         )
 
     def loop(body, first=0, last=heads):
@@ -234,9 +225,8 @@
             mixed_copy(h, index).start()
         gathered[h, lanes(here, HD), :] = mixed[cols(h), lanes(here, share)]
 
-    def arrive(h, slot, level_of, chunk_of):
-        level_of(h).wait_recv()
-        for index in order:
+    def take(h, slot, indices, chunk_of):
+        for index in indices:
             chunk_of(h, index).wait_recv()
             place = lanes(peer_of(index), share)
             mine = stat[h, 0:1, place], acc[h, :, place]
@@ -250,15 +240,39 @@
 
     tile = math.gcd(w_ref.shape[2], 512)
 
-    def project(h, target=None):
+    def multiply(h, rows, target):
+        left = gathered[h, rows, :].T
+        for begin in range(0, w_ref.shape[2], tile):
+            piece = slice(begin, begin + tile)
+            product = jnp.dot(left, w_ref[h, rows, piece], preferred_element_type=F32)
+            target[:, piece] = (summed[:, piece] + product).astype(target.dtype)
+
+    def project(h):
         settle(w_ref.at[h], w_sem.at[h])
         settle(gathered.at[h, pl.ds(0, (peers - 1) * HD)], m_rx.at[h])
-        left = gathered[h].T
-        target = summed if target is None else target
-        for begin in range(0, w_ref.shape[2], tile):
-            piece = slice(begin, begin + tile)
-            product = jnp.dot(left, w_ref[h, :, piece], preferred_element_type=F32)
-            target[:, piece] = (summed[:, piece] + product).astype(target.dtype)
+        multiply(h, pl.ds(0, peers * HD), summed)
+
+    def project_far():
+        settle(w_ref.at[last], w_sem.at[last])
+        if chips > 1:
+            settle(gathered.at[last, pl.ds(0, (peers - 2) * HD)], m_rx.at[last])
+        for hop in range(1, chips):
+            multiply(last, lanes(lax.rem(chip + hop, chips), 2 * HD), summed)
+
+    def project_near():
+        settle(gathered.at[last, pl.ds(0, HD)], m_rx.at[heads])
+        multiply(last, lanes(chip, 2 * HD), out_ref)
+
+    def wind_up(slot, level_of, chunk_of):
+        level_of(inner).wait_recv()
+        take(inner, slot, order[:-2], chunk_of)
+        project(inner - 1)
+        level_of(last).wait_recv()
+        take(last, slot, order[:-1], chunk_of)
+        take(inner, slot, order[-2:], chunk_of)
+        project(inner)
+        project_far()
+        take(last, slot, order[-1:], chunk_of)
 
     def project_before(h):
         pl.when(h > 0)(lambda: project(h - 1))
@@ -273,7 +287,6 @@
     def own_state(h):
         return dot_tn(v_ref[:, cols(h)], k_ref[:, cols(h)])
 
-    last = heads - 1
     later = pl.ds(1, last)
 
     @pl.when(seq == 0)
@@ -308,6 +321,7 @@
         loop(own, 1)
         pl.semaphore_wait(gate.at[0], 1)
         loop(work)
+        project_far()
         settle(k_ref, tx.at[0])
         settle(v_ref, tx.at[1])
         state_copy(last, 1).wait_send()
@@ -355,7 +369,7 @@
             s_send[last] = (s_recv[last].astype(F32) + s_own[last]).astype(BF16)
             state_copy(last, 2).start()
 
-        def work(h, final=False):
+        def work(h, stage=0):
             arrived = kv_copies(h)
             arrived[0].wait_recv()
             for slot in range(2):
@@ -367,7 +381,7 @@
                 pstat[slot, 2:3, :] = recip(total)
                 ebuf[slot] = expo.astype(BF16)
             arrived[1].wait_recv()
-            if final:
+            if stage == 2:
                 early = s_recv[h]
             else:
                 early = early_state(h)
@@ -381,28 +395,39 @@
                 )
                 l_send[slot, h] = bottom
                 o_send[slot, h] = output.astype(BF16)
-                straight = final and slot
+                straight = stage and slot
                 (level_onward(h) if straight else level_copy(h, slot)).start()
-                for index in order[:-2] if final else order:
+                for index in order[:-2] if stage else order:
                     (chunk_onward(h, index) if straight else chunk_copy(h, slot, index)).start()
-            if final:
-                for index in order[-2:]:
-                    chunk_onward(h, index).start()
-                    chunk_copy(h, 0, index).start()
+            if stage == 1:
+                @pl.when(core == 1)
+                def _():
+                    both(h, order[-2:])
+            if stage == 2:
+                both(h, order[-2:-1])
+
+                @pl.when(core == 0)
+                def _():
+                    both(inner, order[-2:])
+
+                both(h, order[-1:])
             else:
-                @pl.when(h == 1)
-                def _():
-                    early_last()
-
+                if not stage:
+                    pl.when(h == 1)(early_last)
                 pre(h + 1)
 
             rest(h, early)
             project(h - 1)
 
-        if last == 1:
-            early_last()
-        loop(work, 1, last)
-        work(last, True)
+        def both(h, indices):
+            for index in indices:
+                chunk_onward(h, index).start()
+                chunk_copy(h, 0, index).start()
+
+        loop(work, 1, inner)
+        work(inner, 1)
+        work(last, 2)
+        project_far()
         for copy in near_copies() + far_copies():
             copy.wait_send()
         settle(s_send.at[later], tx.at[4])
@@ -411,8 +436,11 @@
 
     @pl.when(seq == 2)
     def _():
-        for h in range(1, min(3, heads)):
+        for h in range(1, heads):
             query_copy(h, 0, 1, 0).start()
+        for h in (inner, last):
+            for copy in kv_copies(h, 2, 3):
+                copy.start()
         weights()
 
         def first(h):
@@ -432,23 +460,11 @@
 
         def third(h):
             query_copy(h, 1, 2, 0).wait_recv()
-            if h > 1:
-                relay_copy(h).start()
-                if h + 1 < heads:
-                    query_copy(h + 1, 0, 1, 0).start()
-            if h:
-                bottom, output = part(qbuf[1, :, cols(h)], (pair(h),))
-                if h < heads - 1:
-                    pstat[h, 0:1, :] = bottom
-                    pacc[h] = output
-                else:
-                    l_send[0, h] = bottom
-                    o_send[0, h] = output.astype(BF16)
-                    for copy in part_copies():
-                        copy.start()
-
-        for h in [*range(2, heads), 0]:
-            third(h)
+            bottom, output = part(qbuf[1, :, cols(h)], (pair(h),))
+            pstat[h, 0:1, :] = bottom
+            pacc[h] = output
+
+        query_copy(0, 1, 2, 0).wait_recv()
         for copy in near_copies() + far_copies():
             copy.wait_recv()
         pairs = [(kbuf[:, cols(i)], vbuf[:, cols(i)]) for i in range(2)]
@@ -464,19 +480,19 @@
         query = q_ref[:, cols(0)]
         windowed = blend(current(0), part(query, pairs))[1]
         finish(0, windowed, lin[0] + dot_nt(early.astype(BF16), query))
-        if heads > 2:
-            third(1)
+        loop(third, 1, inner)
 
         def state(h):
             state_copy(h, 2).wait_recv()
             s_send[h] = (s_recv[h].astype(F32) + s_own[h]).astype(BF16)
             state_copy(h, 3).start()
-
             lin[h] = norm(lin[h] + dot_nt(s_recv[h], q_ref[:, cols(h)]))
 
-        def close(h):
-            arrive(h, 0, lambda h: level_copy(h, 0), lambda h, index: chunk_copy(h, 0, index))
-            project(h - 1)
+        def level_here(h):
+            return level_copy(h, 0)
+
+        def chunk_here(h, index):
+            return chunk_copy(h, 0, index)
 
         def second(h):
             state(h)
@@ -497,30 +513,37 @@
                 o_send[1, h, :, place] = output.astype(BF16)
                 chunk_onward(h, index).start()
 
-            @pl.when(h == 1)
-            def _():
-                state(last)
-
-            close(h)
-
-        loop(second, 1, last)
-        close(last)
-        for copy in part_copies():
-            copy.wait_send()
+            pl.when(h == 1)(lambda: state(last))
+            level_here(h).wait_recv()
+            take(h, 0, order, chunk_here)
+            project(h - 1)
+
+        loop(second, 1, inner)
+        state(inner)
+        wind_up(0, level_here, chunk_here)
         settle(q_ref.at[:, pl.ds(HD, width - HD)], tx.at[0])
-        if heads > 2:
-            settle(q_ref.at[:, pl.ds(2 * HD, width - 2 * HD)], tx.at[1])
+        settle(k_ref.at[:, pl.ds(inner * HD, 2 * HD)], tx.at[2])
+        settle(v_ref.at[:, pl.ds(inner * HD, 2 * HD)], tx.at[3])
         settle(s_send, tx.at[4])
-        settle(l_send.at[1, pl.ds(0, heads - 1)], tx.at[5])
-        settle(o_send.at[1, pl.ds(0, heads - 1)], tx.at[6])
+        settle(l_send.at[1, pl.ds(0, inner)], tx.at[5])
+        settle(o_send.at[1, pl.ds(0, inner)], tx.at[6])
 
     @pl.when(seq == 3)
     def _():
-        query_copy(1, 1, 1, 0).start()
-        for h in [*range(2, heads), 0, 1]:
-            query_copy(h, 1, 2, 1).start()
+        for h in range(1, heads):
+            query_copy(h, 1, 1, 0).start()
+            if 1 < h <= inner + 1:
+                query_copy(h - 2, 1, 2, 1).start()
         weights()
         loop(own)
+        for h in (inner, last):
+            for copy in kv_copies(h, 2, 3):
+                copy.wait_recv()
+            bottom, output = blend(
+                current(h), part(q_ref[:, cols(h)], ((kbuf[:, cols(h)], vbuf[:, cols(h)]),))
+            )
+            stat[h, 0:1, :] = bottom
+            acc[h] = output
 
         def state(h):
             state_copy(h, 3).wait_recv()
@@ -528,22 +551,18 @@
 
         def work(h):
             state(h)
-            arrive(h, 1, level_onward, chunk_onward)
+            level_onward(h).wait_recv()
+            take(h, 1, order, chunk_onward)
             project_before(h)
 
-        loop(work, 0, last)
+        loop(work, 0, inner)
         state(last)
-        for copy in part_copies():
-            copy.wait_recv()
-        bottom, output = blend(current(last), (l_recv[0, last], o_recv[0, last].astype(F32)))
-        stat[last, 0:1, :] = bottom
-        acc[last] = output
-        arrive(last, 1, level_onward, chunk_onward)
-        project(last - 1)
-        query_copy(1, 1, 1, 0).wait_send()
-        settle(q_ref, tx.at[1])
-
-    project(heads - 1, out_ref)
+        state(inner)
+        wind_up(1, level_onward, chunk_onward)
+        settle(q_ref.at[:, pl.ds(HD, width - HD)], tx.at[0])
+        settle(q_ref.at[:, pl.ds(0, inner * HD)], tx.at[1])
+
+    project_near()
     settle(mixed.at[:, pl.ds(0, length - share)], tx.at[8])
 
 
@@ -584,7 +603,7 @@
             pltpu.VMEM((width, length), BF16),
             pltpu.VMEM((heads, peers * HD, share), BF16),
             dma((3,)), dma((heads,)), dma((9,)), dma((2, heads)), dma((2, heads)),
-            dma((2 * (heads - 1), peers)), dma((2 * (heads - 1),)), dma((heads,)), dma((heads,)),
+            dma((2 * (heads - 1), peers)), dma((2 * (heads - 1),)), dma((heads,)), dma((heads + 1,)),
             pltpu.SemaphoreType.REGULAR((2,)),
         ],
         compiler_params=pltpu.CompilerParams(
@@ -603,7 +622,7 @@
     length, width = queries.shape
     blocks = lax.axis_size("seq")
     share = length // lax.axis_size("head")
-    whole = share % HD == 0 and width % HD == 0 and width > HD and lax.axis_size("head") % 2 == 0
+    whole = share % HD == 0 and width % HD == 0 and width >= 4 * HD and lax.axis_size("head") % 2 == 0
     return blocks == 4 and blocks * length <= WINDOW and whole
 
 

time: 37.5 us -> 38 us (1.013)
  the two profiles are of different devices: /device:TPU:17 before, /device:TPU:25 now
where the time goes in v5:
time: 38 us; the launch traced here: 37.4 us
  Pallas kernels  36.6 us (96%)
  local copies, waits for them, and re-layouts  0.8 us (2%)
    pallas_call x1, Pallas kernels, fused(): pl.pallas_call(functools.partial(kernel, peers), out_shape=pltpu.VMEM((sh...  36.6 us
    unnamed x1, local copies, waits for them, and re-layouts  0.8 us

profile of v5, /device:TPU:25, one launch (start us, length us, event | category | flops | bytes accessed | tf_op | source)
XLA Modules:
  0.0 37.4 jit_solution(8182484397227095481)
XLA Ops:
  0.0 36.6 %shard_map.46 = bf16[128,2048]{1,0:T(8,128)(2,1)S(1)} custom-call(bf16[512,512]{1,0:T(8,128)(2,1)} %q_hbm.1, bf16[512,512]{1,0:T(8,128)(2,1)} %k_hbm.1, bf16[512,512]{1,0:T(8,128)(2,1)} %v_hbm.1, bf16[2048,2048]{1,0:T(8,128)(2,1)} %w_hbm.1), custom_call_target="tpu_custom_call" | custom-call | tf_op jit(solution)/shard_map/pallas_call | solution.py:576
  36.6 0.8 %copy.6 = bf16[128,2048]{1,0:T(8,128)(2,1)} copy(bf16[128,2048]{1,0:T(8,128)(2,1)S(1)} %shard_map.46) | data formatting | bytes 1048576

commit v6 on v5

--- a/solution.py
+++ b/solution.py
@@ -530,10 +530,12 @@
 
     @pl.when(seq == 3)
     def _():
-        for h in range(1, heads):
+        query_copy(1, 1, 1, 0).start()
+        query_copy(0, 1, 2, 1).start()
+        for h in range(2, heads):
             query_copy(h, 1, 1, 0).start()
-            if 1 < h <= inner + 1:
-                query_copy(h - 2, 1, 2, 1).start()
+            if h <= inner:
+                query_copy(h - 1, 1, 2, 1).start()
         weights()
         loop(own)
         for h in (inner, last):

time: 38 us -> 36.3 us (0.955)
  the two profiles are of different devices: /device:TPU:25 before, /device:TPU:17 now
where the time goes in v6:
time: 36.3 us; the launch traced here: 36.2 us
  Pallas kernels  35.4 us (98%)
  local copies, waits for them, and re-layouts  0.8 us (2%)
    pallas_call x1, Pallas kernels, fused(): pl.pallas_call(functools.partial(kernel, peers), out_shape=pltpu.VMEM((sh...  35.4 us
    unnamed x1, local copies, waits for them, and re-layouts  0.8 us

profile of v6, /device:TPU:17, one launch (start us, length us, event | category | flops | bytes accessed | tf_op | source)
XLA Modules:
  0.0 36.2 jit_solution(325509439949748415)
XLA Ops:
  0.0 35.4 %shard_map.46 = bf16[128,2048]{1,0:T(8,128)(2,1)S(1)} custom-call(bf16[512,512]{1,0:T(8,128)(2,1)} %q_hbm.1, bf16[512,512]{1,0:T(8,128)(2,1)} %k_hbm.1, bf16[512,512]{1,0:T(8,128)(2,1)} %v_hbm.1, bf16[2048,2048]{1,0:T(8,128)(2,1)} %w_hbm.1), custom_call_target="tpu_custom_call" | custom-call | tf_op jit(solution)/shard_map/pallas_call | solution.py:578
  35.4 0.8 %copy.6 = bf16[128,2048]{1,0:T(8,128)(2,1)} copy(bf16[128,2048]{1,0:T(8,128)(2,1)S(1)} %shard_map.46) | data formatting | bytes 1048576

commit v7 on v6

--- a/solution.py
+++ b/solution.py
@@ -82,7 +82,7 @@
         return pltpu.make_async_copy(
             w_hbm.at[pl.ds(pl.multiple_of(peer * width + h * HD, HD), HD), :],
             w_ref.at[h, pl.ds(peer * HD, HD), :],
-            w_sem.at[h],
+            w_sem.at[0],
         )
 
     def load_head(h):
@@ -170,7 +170,7 @@
         target = peer_of(index)
         return remote(
             mixed.at[cols(h), lanes(target, share)], gathered.at[h, lanes(here, HD), :],
-            8, m_rx.at[h + h // last if index == 1 else h], {"head": target},
+            8, m_rx.at[h], {"head": target},
         )
 
     def loop(body, first=0, last=heads):
@@ -240,28 +240,15 @@
 
     tile = math.gcd(w_ref.shape[2], 512)
 
-    def multiply(h, rows, target):
+    def project(h, target=None):
+        settle(gathered.at[h, pl.ds(0, (peers - 1) * HD)], m_rx.at[h])
+        rows = pl.ds(0, peers * HD)
         left = gathered[h, rows, :].T
+        target = summed if target is None else target
         for begin in range(0, w_ref.shape[2], tile):
             piece = slice(begin, begin + tile)
             product = jnp.dot(left, w_ref[h, rows, piece], preferred_element_type=F32)
             target[:, piece] = (summed[:, piece] + product).astype(target.dtype)
-
-    def project(h):
-        settle(w_ref.at[h], w_sem.at[h])
-        settle(gathered.at[h, pl.ds(0, (peers - 1) * HD)], m_rx.at[h])
-        multiply(h, pl.ds(0, peers * HD), summed)
-
-    def project_far():
-        settle(w_ref.at[last], w_sem.at[last])
-        if chips > 1:
-            settle(gathered.at[last, pl.ds(0, (peers - 2) * HD)], m_rx.at[last])
-        for hop in range(1, chips):
-            multiply(last, lanes(lax.rem(chip + hop, chips), 2 * HD), summed)
-
-    def project_near():
-        settle(gathered.at[last, pl.ds(0, HD)], m_rx.at[heads])
-        multiply(last, lanes(chip, 2 * HD), out_ref)
 
     def wind_up(slot, level_of, chunk_of):
         level_of(inner).wait_recv()
@@ -271,7 +258,6 @@
         take(last, slot, order[:-1], chunk_of)
         take(inner, slot, order[-2:], chunk_of)
         project(inner)
-        project_far()
         take(last, slot, order[-1:], chunk_of)
 
     def project_before(h):
@@ -320,8 +306,8 @@
         weights()
         loop(own, 1)
         pl.semaphore_wait(gate.at[0], 1)
+        settle(w_ref, w_sem.at[0])
         loop(work)
-        project_far()
         settle(k_ref, tx.at[0])
         settle(v_ref, tx.at[1])
         state_copy(last, 1).wait_send()
@@ -361,6 +347,7 @@
             onward.start()
         pl.semaphore_wait(gate.at[0], 1)
         tell(0, {"seq": 0})
+        settle(w_ref, w_sem.at[0])
         rest(0, early_state(0).astype(BF16))
         pre(1)
 
@@ -397,14 +384,15 @@
                 o_send[slot, h] = output.astype(BF16)
                 straight = stage and slot
                 (level_onward(h) if straight else level_copy(h, slot)).start()
-                for index in order[:-2] if stage else order:
-                    (chunk_onward(h, index) if straight else chunk_copy(h, slot, index)).start()
+                if stage < 2:
+                    for index in order[:-2] if stage else order:
+                        (chunk_onward(h, index) if straight else chunk_copy(h, slot, index)).start()
             if stage == 1:
                 @pl.when(core == 1)
                 def _():
                     both(h, order[-2:])
             if stage == 2:
-                both(h, order[-2:-1])
+                both(h, order[:-1])
 
                 @pl.when(core == 0)
                 def _():
@@ -421,13 +409,12 @@
 
         def both(h, indices):
             for index in indices:
+                chunk_copy(h, 0, index).start()
                 chunk_onward(h, index).start()
-                chunk_copy(h, 0, index).start()
 
         loop(work, 1, inner)
         work(inner, 1)
         work(last, 2)
-        project_far()
         for copy in near_copies() + far_copies():
             copy.wait_send()
         settle(s_send.at[later], tx.at[4])
@@ -465,6 +452,7 @@
             pacc[h] = output
 
         query_copy(0, 1, 2, 0).wait_recv()
+        settle(w_ref, w_sem.at[0])
         for copy in near_copies() + far_copies():
             copy.wait_recv()
         pairs = [(kbuf[:, cols(i)], vbuf[:, cols(i)]) for i in range(2)]
@@ -557,6 +545,7 @@
             take(h, 1, order, chunk_onward)
             project_before(h)
 
+        settle(w_ref, w_sem.at[0])
         loop(work, 0, inner)
         state(last)
         state(inner)
@@ -564,7 +553,7 @@
         settle(q_ref.at[:, pl.ds(HD, width - HD)], tx.at[0])
         settle(q_ref.at[:, pl.ds(0, inner * HD)], tx.at[1])
 
-    project_near()
+    project(last, out_ref)
     settle(mixed.at[:, pl.ds(0, length - share)], tx.at[8])
 
 
@@ -604,8 +593,8 @@
             pltpu.VMEM((heads, 8, length), F32),
             pltpu.VMEM((width, length), BF16),
             pltpu.VMEM((heads, peers * HD, share), BF16),
-            dma((3,)), dma((heads,)), dma((9,)), dma((2, heads)), dma((2, heads)),
-            dma((2 * (heads - 1), peers)), dma((2 * (heads - 1),)), dma((heads,)), dma((heads + 1,)),
+            dma((3,)), dma((1,)), dma((9,)), dma((2, heads)), dma((2, heads)),
+            dma((2 * (heads - 1), peers)), dma((2 * (heads - 1),)), dma((heads,)), dma((heads,)),
             pltpu.SemaphoreType.REGULAR((2,)),
         ],
         compiler_params=pltpu.CompilerParams(

time: 36.3 us -> 35.9 us (0.989)
  the two profiles are of different devices: /device:TPU:17 before, /device:TPU:25 now
where the time goes in v7:
time: 35.9 us; the launch traced here: 35.8 us
  Pallas kernels  35 us (97%)
  local copies, waits for them, and re-layouts  0.8 us (2%)
    pallas_call x1, Pallas kernels, fused(): pl.pallas_call(functools.partial(kernel, peers), out_shape=pltpu.VMEM((sh...  35 us
    unnamed x1, local copies, waits for them, and re-layouts  0.8 us

profile of v7, /device:TPU:25, one launch (start us, length us, event | category | flops | bytes accessed | tf_op | source)
XLA Modules:
  0.0 35.8 jit_solution(481909590286149676)
XLA Ops:
  0.0 35.0 %shard_map.46 = bf16[128,2048]{1,0:T(8,128)(2,1)S(1)} custom-call(bf16[512,512]{1,0:T(8,128)(2,1)} %q_hbm.1, bf16[512,512]{1,0:T(8,128)(2,1)} %k_hbm.1, bf16[512,512]{1,0:T(8,128)(2,1)} %v_hbm.1, bf16[2048,2048]{1,0:T(8,128)(2,1)} %w_hbm.1), custom_call_target="tpu_custom_call" | custom-call | tf_op jit(solution)/shard_map/pallas_call | solution.py:567
  35.0 0.8 %copy.6 = bf16[128,2048]{1,0:T(8,128)(2,1)} copy(bf16[128,2048]{1,0:T(8,128)(2,1)S(1)} %shard_map.46) | data formatting | bytes 1048576

commit v8 on v7

--- a/solution.py
+++ b/solution.py
@@ -399,13 +399,12 @@
                     both(inner, order[-2:])
 
                 both(h, order[-1:])
-            else:
-                if not stage:
-                    pl.when(h == 1)(early_last)
-                pre(h + 1)
-
+            elif not stage:
+                pl.when(h == 1)(early_last)
             rest(h, early)
             project(h - 1)
+            if stage < 2:
+                pre(h + 1)
 
         def both(h, indices):
             for index in indices:

time: 35.9 us -> 35.9 us (level)
  no operation moved by 1% of the time
where the time goes in v8:
time: 35.9 us; the launch traced here: 35.8 us
  Pallas kernels  35 us (97%)
  local copies, waits for them, and re-layouts  0.8 us (2%)
    pallas_call x1, Pallas kernels, fused(): pl.pallas_call(functools.partial(kernel, peers), out_shape=pltpu.VMEM((sh...  35 us
    unnamed x1, local copies, waits for them, and re-layouts  0.8 us

profile of v8, /device:TPU:25, one launch (start us, length us, event | category | flops | bytes accessed | tf_op | source)
XLA Modules:
  0.0 35.8 jit_solution(8920309891248887441)
XLA Ops:
  0.0 35.0 %shard_map.46 = bf16[128,2048]{1,0:T(8,128)(2,1)S(1)} custom-call(bf16[512,512]{1,0:T(8,128)(2,1)} %q_hbm.1, bf16[512,512]{1,0:T(8,128)(2,1)} %k_hbm.1, bf16[512,512]{1,0:T(8,128)(2,1)} %v_hbm.1, bf16[2048,2048]{1,0:T(8,128)(2,1)} %w_hbm.1), custom_call_target="tpu_custom_call" | custom-call | tf_op jit(solution)/shard_map/pallas_call | solution.py:566
  35.0 0.8 %copy.6 = bf16[128,2048]{1,0:T(8,128)(2,1)} copy(bf16[128,2048]{1,0:T(8,128)(2,1)S(1)} %shard_map.46) | data formatting | bytes 1048576

commit v9 on v8

--- a/solution.py
+++ b/solution.py
@@ -37,7 +37,7 @@
     peers, q_hbm, k_hbm, v_hbm, w_hbm, out_ref, q_ref, k_ref, v_ref,
     w_ref, summed, kbuf, vbuf, qbuf, ebuf, pacc, pstat, o_send, o_recv, l_send, l_recv,
     s_own, s_send, s_recv, acc, lin, stat, mixed, gathered,
-    in_sem, w_sem, tx, kv_rx, q_rx, o_rx, l_rx, s_rx, m_rx, gate,
+    tx, kv_rx, q_rx, o_rx, l_rx, s_rx, m_rx, gate,
 ):
     seq = lax.axis_index("seq")
     here = lax.axis_index("head")
@@ -72,7 +72,7 @@
                 greet({"head": peer_of(index)})
 
     loads = [
-        pltpu.make_async_copy(source, target, in_sem.at[i])
+        pltpu.make_async_copy(source, target, tx.at[i])
         for i, (source, target) in enumerate(((q_hbm, q_ref), (k_hbm, k_ref), (v_hbm, v_ref)))
     ]
     for load in loads:
@@ -82,7 +82,7 @@
         return pltpu.make_async_copy(
             w_hbm.at[pl.ds(pl.multiple_of(peer * width + h * HD, HD), HD), :],
             w_ref.at[h, pl.ds(peer * HD, HD), :],
-            w_sem.at[0],
+            tx.at[8],
         )
 
     def load_head(h):
@@ -306,7 +306,7 @@
         weights()
         loop(own, 1)
         pl.semaphore_wait(gate.at[0], 1)
-        settle(w_ref, w_sem.at[0])
+        settle(w_ref, tx.at[8])
         loop(work)
         settle(k_ref, tx.at[0])
         settle(v_ref, tx.at[1])
@@ -347,7 +347,7 @@
             onward.start()
         pl.semaphore_wait(gate.at[0], 1)
         tell(0, {"seq": 0})
-        settle(w_ref, w_sem.at[0])
+        settle(w_ref, tx.at[8])
         rest(0, early_state(0).astype(BF16))
         pre(1)
 
@@ -451,7 +451,7 @@
             pacc[h] = output
 
         query_copy(0, 1, 2, 0).wait_recv()
-        settle(w_ref, w_sem.at[0])
+        settle(w_ref, tx.at[8])
         for copy in near_copies() + far_copies():
             copy.wait_recv()
         pairs = [(kbuf[:, cols(i)], vbuf[:, cols(i)]) for i in range(2)]
@@ -544,7 +544,7 @@
             take(h, 1, order, chunk_onward)
             project_before(h)
 
-        settle(w_ref, w_sem.at[0])
+        settle(w_ref, tx.at[8])
         loop(work, 0, inner)
         state(last)
         state(inner)
@@ -592,8 +592,8 @@
             pltpu.VMEM((heads, 8, length), F32),
             pltpu.VMEM((width, length), BF16),
             pltpu.VMEM((heads, peers * HD, share), BF16),
-            dma((3,)), dma((1,)), dma((9,)), dma((2, heads)), dma((2, heads)),
-            dma((2 * (heads - 1), peers)), dma((2 * (heads - 1),)), dma((heads,)), dma((heads,)),
+            dma((9,)), dma((2, heads)), dma((2, heads)),
+            dma((2 * heads - 4, peers)), dma((2 * heads - 4,)), dma((heads,)), dma((heads,)),
             pltpu.SemaphoreType.REGULAR((2,)),
         ],
         compiler_params=pltpu.CompilerParams(

time: 35.9 us -> 35.8 us (level)
  no operation moved by 1% of the time
where the time goes in v9:
time: 35.8 us; the launch traced here: 35.7 us
  Pallas kernels  34.9 us (97%)
  local copies, waits for them, and re-layouts  0.8 us (2%)
    pallas_call x1, Pallas kernels, fused(): pl.pallas_call(functools.partial(kernel, peers), out_shape=pltpu.VMEM((sh...  34.9 us
    unnamed x1, local copies, waits for them, and re-layouts  0.8 us

profile of v9, /device:TPU:25, one launch (start us, length us, event | category | flops | bytes accessed | tf_op | source)
XLA Modules:
  0.0 35.7 jit_solution(17686760389938184931)
XLA Ops:
  0.0 34.9 %shard_map.46 = bf16[128,2048]{1,0:T(8,128)(2,1)S(1)} custom-call(bf16[512,512]{1,0:T(8,128)(2,1)} %q_hbm.1, bf16[512,512]{1,0:T(8,128)(2,1)} %k_hbm.1, bf16[512,512]{1,0:T(8,128)(2,1)} %v_hbm.1, bf16[2048,2048]{1,0:T(8,128)(2,1)} %w_hbm.1), custom_call_target="tpu_custom_call" | custom-call | tf_op jit(solution)/shard_map/pallas_call | solution.py:566
  34.9 0.8 %copy.6 = bf16[128,2048]{1,0:T(8,128)(2,1)} copy(bf16[128,2048]{1,0:T(8,128)(2,1)S(1)} %shard_map.46) | data formatting | bytes 1048576
